TPU v7x, 32 devices: a whole 2x2x4 slice. The times are simulated.
32 devices in a mesh: draws: 2 (over y), dst: 4 (over z), org: 2 (over x), st: 2 (over core).
Axes of the slice: x: 2, y: 2, z: 4, core: 2. Of those that a mesh axis runs over, the one named last changes fastest.
Arguments:
- value_now: float32 [8, 2, 64, 4096], P(('draws', 'dst'), 'org', None, 'st'), parts along dimension 0, may hold values from -90 to 490
- utility: float32 [8, 2, 64, 4096], P(('draws', 'dst'), 'org', None, 'st'), parts along dimension 0, may hold values from -6 to 6
- move_costs: float32 [8, 2, 64, 4, 128], P('draws', 'org', None, 'dst'), parts along dimension 0, may hold values from 0 to 3
- dest_blocks: int32 [8, 3], replicated, may hold values from 0 to 7, all different within a row
- row_counts: int32 [8], replicated, may hold values from 1 to 3, as said below
- transition: int32 [4096], replicated, may hold values from 0 to 4095
Outputs:
- value_next: float32 [8, 2, 64, 4096], P(('draws', 'dst'), 'org', None, 'st'), parts along dimension 0
There are 2 independent parts, one for each index of `draws`. A program takes and returns all parts, laid end to end along the dimension named above; an argument that names none is the same for every part. Nothing has to cross between parts.
Inputs may be any that keep to these rules, and one draw needn't show every extreme that they name: `dest_blocks`: each row names 3 different blocks; only the first row_counts[o] of row o count. `row_counts`: some anchor block has 3.
All inputs are finite; a program needn't handle non-finite values.
Results may differ from a plain program's by a relative error of at most 0.00095.
Values may be sent and summed in bfloat16 or wider, within the bound.
No kernel may reach another device: no remote copies, remote signals or barrier semaphores. Data moves between devices by JAX's collectives and lax.ppermute only.
A program may use at most 64 MiB of HBM per device.

v0:
```python
import jax
import jax.numpy as jnp
from jax import lax
from jax.sharding import PartitionSpec as P

DISCOUNT = 0.95
FLOOR = -1e30


def block_terms(kernel, feasible, ceiling, dest_piece):
    pieces = dest_piece.shape[0]
    block_rows = dest_piece.shape[1]
    states = dest_piece.shape[2]
    dest_rows = dest_piece.reshape(pieces * block_rows, states)

    def dense_anchor(operands):
        kernel_row, usable_row, ceiling_row = operands
        keep_mask = jnp.broadcast_to(usable_row[:, None], (pieces, block_rows)).reshape(
            pieces * block_rows, 1
        )
        weights = jnp.where(keep_mask, jnp.exp(dest_rows - ceiling_row[None, :]), 0.0).astype(
            jnp.bfloat16
        )
        return jnp.dot(kernel_row, weights, preferred_element_type=jnp.float32)

    return lax.map(dense_anchor, (kernel, feasible, ceiling))


def on_device(value_now, utility, move_costs, dest_blocks, row_counts, transition):
    dest_groups = lax.axis_size("dst")
    orig_groups = lax.axis_size("org")
    dest_index = lax.axis_index("dst")
    orig_index = lax.axis_index("org")
    state_index = lax.axis_index("st")
    states = value_now.shape[3]
    slot_count = dest_blocks.shape[1]
    every_state = lax.all_gather(value_now, "st", axis=3, tiled=True)
    chosen = lax.dynamic_slice_in_dim(transition, state_index * states, states)
    shifted = jnp.take(every_state, chosen, axis=3)
    own_piece = shifted[0]
    kernel = jnp.exp(-move_costs[:, 0, :, 0, :]).astype(jnp.bfloat16)
    lists_by = dest_blocks.reshape(dest_groups, orig_groups, slot_count)
    counts_by = row_counts.reshape(dest_groups, orig_groups)
    lists_mine = lax.dynamic_index_in_dim(lists_by, orig_index, 1, keepdims=False)
    counts_mine = lax.dynamic_index_in_dim(counts_by, orig_index, 1, keepdims=False)
    slot_ids = jnp.arange(slot_count, dtype=jnp.int32)
    usable = slot_ids[None, :] < counts_mine[:, None]
    dest_ids = dest_index * orig_groups + jnp.arange(orig_groups, dtype=jnp.int32)
    feasible = jnp.any(
        (lists_mine[:, :, None] == dest_ids[None, None, :]) & usable[:, :, None], axis=1
    )
    own_id = dest_index * orig_groups + orig_index
    slot_live = slot_ids[None, :] < row_counts[:, None]
    reaches = jnp.any((dest_blocks == own_id) & slot_live, axis=1)
    own_top = jnp.max(own_piece[0], axis=0)
    offered = jnp.where(reaches[:, None], own_top[None, :], FLOOR)
    every_top = lax.pmax(offered.astype(jnp.bfloat16), ("dst", "org")).astype(offered.dtype)
    ceiling = lax.dynamic_index_in_dim(
        every_top.reshape(dest_groups, orig_groups, states), orig_index, 1, keepdims=False
    )
    partial_value = block_terms(
        kernel, feasible, ceiling, lax.all_gather(own_piece, "org", axis=0, tiled=True)
    )
    rounded = partial_value.astype(jnp.bfloat16)
    merged = jnp.sum(
        lax.all_to_all(rounded, "dst", split_axis=0, concat_axis=0, tiled=True),
        axis=0,
        dtype=jnp.float32,
    )
    own_ceiling = lax.dynamic_index_in_dim(ceiling, dest_index, 0, keepdims=False)
    result = utility[0, 0] + DISCOUNT * (own_ceiling[None, :] + jnp.log(merged))
    return result[None, None]


def solution(mesh):
    return jax.shard_map(
        on_device,
        mesh=mesh,
        in_specs=(
            P(("draws", "dst"), "org", None, "st"),
            P(("draws", "dst"), "org", None, "st"),
            P("draws", "org", None, "dst", None),
            P(),
            P(),
            P(),
        ),
        out_specs=P(("draws", "dst"), "org", None, "st"),
        check_vma=False,
    )
```

profile of v0, /device:TPU:0, one launch (start us, length us, event | category | flops | bytes accessed | tf_op | source)
XLA Modules:
  0.0 111.2 jit_solution(2827117173432948598)
XLA Ops:
  6.5 0.0 all-gather.3.cloned.1.call-start
  6.5 2.4 %copy.18 = f32[1,1,64,2048]{2,3,1,0:T(8,128)} copy(f32[1,1,64,2048]{3,2,1,0:T(8,128)} %param.8) | data formatting | bytes 1048576 | tf_op args[0]
  8.9 0.0 all-gather.3.cloned.1.call-update
  9.0 0.0 all-gather.5.cloned.1.call-start
  9.0 0.0 copy-done.4
  9.1 0.1 reshape.142
  9.1 0.0 copy-done.3
  9.1 0.1 copy.20
  9.2 0.2 dynamic-slice_reduce_fusion
  9.4 0.0 copy-done.2
  9.5 0.1 iota_compare_fusion
  9.6 0.2 and_reduce_fusion
  9.8 12.6 %all-gather.3.cloned.1.call-done = f32[1,1,64,4096]{2,3,1,0:T(8,128)} async-done(((f32[1,1,64,2048]{2,3,1,0:T(8,128)}), f32[1,1,64,4096]{2,3,1,0:T(8,128)}) %all-gather.3.cloned.1.call-update) | async-done | bytes 1048592 | tf_op jit(solution)/shard_map/all_gather | solution.py:37
  22.4 7.0 %gather_fusion = f32[2048,64]{1,0:T(8,128)S(1)} fusion(f32[64,4096]{0,1:T(8,128)} %bitcast.42, s32[2048]{0:T(1024)S(1)} %fusion.12), kind=kCustom, calls=%fused_computation | custom fusion | bytes 1056768 | tf_op jit(solution)/shard_map/jit(_take)/gather | solution.py:39
  29.5 0.0 copy-start.1
  29.5 0.3 bitcast_select_fusion
  29.8 1.1 %copy.21 = f32[1,64,2048]{2,1,0:T(8,128)} copy(f32[1,64,2048]{1,2,0:T(8,128)S(1)} %bitcast_select_fusion) | data formatting | bytes 1048576 | tf_op jit(solution)/shard_map/jit(_take)/select_n | solution.py:39
  30.9 0.0 all-gather.5.cloned.1.call-update
  31.0 0.0 copy-done.1
  31.0 0.6 fusion.8
  31.7 0.1 select_convert_fusion.2
  31.8 37.6 %pmax.7 = bf16[4,2,2048]{2,1,0:T(2,128)(2,1)S(1)} all-reduce(bf16[4,2,2048]{2,1,0:T(2,128)(2,1)S(1)} %reshape.139), channel_id=1, replica_groups=mesh['draws'=2,'dst'=4,'org'=2,'st'=2] {'dst','org'}, use_global_device_ids=true, to_apply=%region_2.3 | all-reduce | flops 16384 | bytes 65536 | tf_op jit(solution)/shard_map/pmax | solution.py:57
  69.4 0.0 all-gather.5.cloned.1.call-done
  69.5 10.5 %while.10 = (s32[]{:T(128)}, bf16[4,64,2048]{2,1,0:T(8,128)(2,1)}, bf16[4,64,128]{2,1,0:T(8,128)(2,1)S(1)}, pred[4,2]{0,1:T(4,128)(4,1)S(1)}, f32[4,2048]{1,0:T(4,128)S(1)}, /*index=5*/f32[128,2048]{1,0:T(8,128)}, s32[]{:T(128)}) while((s32[]{:T(128)}, bf16[4,64,2048]{2,1,0:T(8,128)(2,1)}, bf16[4,64,128]{2,1,0:T(8,128)(2,1)S(1)}, ...), condition=%wide.region_5.6_spmd, body=%wide.region_4.5_spmd.sunk | while | flops 34340864 | bytes 1615847 | solution.py:26
  69.5 0.1 constant_dynamic-slice_fusion.8
  69.6 0.1 copy.28
  69.7 0.1 broadcast_in_dim.107
  69.7 0.1 broadcast_in_dim.108
  69.9 2.3 %fusion.18 = bf16[4,64,2048]{2,1,0:T(8,128)(2,1)} fusion(bf16[4,64,2048]{2,1,0:T(8,128)(2,1)} %get-tuple-element.101, s32[]{:T(128)S(6)} %copy.32, f32[128,2048]{1,0:T(8,128)} %get-tuple-element.112, f32[2048]{0:T(1024)S(1)} %bitcast.43, pred[128]{0:T(512)(128)(4,1)S(1)} %broadcast_in_dim.108, bf16[4,64,128]{2,1,0:T(8,128)(2,1)S(1)} %get-tuple-element.109), kind=kOutput, calls=%fused_computation.2.clone.1 | convolution fusion | flops 34340864 | bytes 1598976 | tf_op jit(solution)/shard_map/while/body/eval_jaxpr/dot_general | solution.py:24
  72.1 0.1 constant_dynamic-slice_fusion.8
  72.2 0.1 copy.28
  72.3 0.1 broadcast_in_dim.107
  72.4 0.1 broadcast_in_dim.108
  72.5 2.2 %fusion.18 = bf16[4,64,2048]{2,1,0:T(8,128)(2,1)} fusion(bf16[4,64,2048]{2,1,0:T(8,128)(2,1)} %get-tuple-element.101, s32[]{:T(128)S(6)} %copy.32, f32[128,2048]{1,0:T(8,128)} %get-tuple-element.112, f32[2048]{0:T(1024)S(1)} %bitcast.43, pred[128]{0:T(512)(128)(4,1)S(1)} %broadcast_in_dim.108, bf16[4,64,128]{2,1,0:T(8,128)(2,1)S(1)} %get-tuple-element.109), kind=kOutput, calls=%fused_computation.2.clone.1 | convolution fusion | flops 34340864 | bytes 1598976 | tf_op jit(solution)/shard_map/while/body/eval_jaxpr/dot_general | solution.py:24
  74.7 0.1 constant_dynamic-slice_fusion.8
  74.8 0.1 copy.28
  74.9 0.1 broadcast_in_dim.107
  75.0 0.1 broadcast_in_dim.108
  75.1 2.2 %fusion.18 = bf16[4,64,2048]{2,1,0:T(8,128)(2,1)} fusion(bf16[4,64,2048]{2,1,0:T(8,128)(2,1)} %get-tuple-element.101, s32[]{:T(128)S(6)} %copy.32, f32[128,2048]{1,0:T(8,128)} %get-tuple-element.112, f32[2048]{0:T(1024)S(1)} %bitcast.43, pred[128]{0:T(512)(128)(4,1)S(1)} %broadcast_in_dim.108, bf16[4,64,128]{2,1,0:T(8,128)(2,1)S(1)} %get-tuple-element.109), kind=kOutput, calls=%fused_computation.2.clone.1 | convolution fusion | flops 34340864 | bytes 1598976 | tf_op jit(solution)/shard_map/while/body/eval_jaxpr/dot_general | solution.py:24
  77.3 0.1 constant_dynamic-slice_fusion.8
  77.4 0.1 copy.28
  77.5 0.1 broadcast_in_dim.107
  77.6 0.1 broadcast_in_dim.108
  77.7 2.3 %fusion.18 = bf16[4,64,2048]{2,1,0:T(8,128)(2,1)} fusion(bf16[4,64,2048]{2,1,0:T(8,128)(2,1)} %get-tuple-element.101, s32[]{:T(128)S(6)} %copy.32, f32[128,2048]{1,0:T(8,128)} %get-tuple-element.112, f32[2048]{0:T(1024)S(1)} %bitcast.43, pred[128]{0:T(512)(128)(4,1)S(1)} %broadcast_in_dim.108, bf16[4,64,128]{2,1,0:T(8,128)(2,1)S(1)} %get-tuple-element.109), kind=kOutput, calls=%fused_computation.2.clone.1 | convolution fusion | flops 34340864 | bytes 1598976 | tf_op jit(solution)/shard_map/while/body/eval_jaxpr/dot_general | solution.py:24
  79.9 3.6 %all-to-all-start = ((bf16[4,64,2048]{2,1,0:T(8,128)(2,1)}), bf16[4,64,2048]{2,1,0:T(8,128)(2,1)S(1)}, u32[]{:S(2)}, u32[]{:S(2)}) async-start(bf16[4,64,2048]{2,1,0:T(8,128)(2,1)} %get-tuple-element.37), calls=%async_computation | async-start | bytes 2097152 | tf_op jit(solution)/shard_map/all_to_all | solution.py:66
  83.6 19.7 %all-to-all-done = bf16[4,64,2048]{2,1,0:T(8,128)(2,1)S(1)} async-done(((bf16[4,64,2048]{2,1,0:T(8,128)(2,1)}), bf16[4,64,2048]{2,1,0:T(8,128)(2,1)S(1)}, u32[]{:S(2)}, u32[]{:S(2)}) %all-to-all-start) | async-done | bytes 1048608 | tf_op jit(solution)/shard_map/all_to_all | solution.py:66
  103.3 0.2 convert_reduce_fusion
  103.5 0.9 fusion.10
  (21 shorter events, 0.3 us)
Async XLA Ops:
  6.5 2.5 %copy-start.4 = (s32[8]{0:T(128)S(1)}, s32[8]{0:T(128)}, u32[]{:S(2)}) copy-start(s32[8]{0:T(128)} %param.12) | copy-start | bytes 100
  6.5 2.6 %copy-start.3 = (s32[8,3]{0,1:T(4,128)S(1)}, s32[8,3]{0,1:T(4,128)}, u32[]{:S(2)}) copy-start(s32[8,3]{0,1:T(4,128)} %param.11) | copy-start | bytes 292
  6.5 2.9 %copy-start.2 = (s32[4096]{0:T(1024)S(1)}, s32[4096]{0:T(1024)}, u32[]{:S(2)}) copy-start(s32[4096]{0:T(1024)} %param.13) | copy-start | bytes 49156
  6.5 15.9 %all-gather.3.cloned.1.call-start = ((), (), s32[]{:S(2)}) async-start(), calls=%async_computation.1 | async-start | bytes 3145728 | tf_op jit(solution)/shard_map/all_gather | solution.py:37
  9.0 60.5 %all-gather.5.cloned.1.call-start = ((), (), s32[]{:S(2)}) async-start(), calls=%async_computation.2 | async-start | bytes 1572864 | tf_op jit(solution)/shard_map/all_gather | solution.py:62
  29.5 1.5 %copy-start.1 = (f32[4,1,64,1,128]{4,3,2,1,0:T(1,128)S(1)}, f32[4,1,64,1,128]{4,3,2,1,0:T(1,128)}, u32[]{:S(2)}) copy-start(f32[4,1,64,1,128]{4,3,2,1,0:T(1,128)} %param.10) | copy-start | bytes 393220
  79.9 23.5 %copy-start = (f32[1,1,64,2048]{3,2,1,0:T(8,128)S(1)}, f32[1,1,64,2048]{3,2,1,0:T(8,128)}, u32[]{:S(2)}) copy-start(f32[1,1,64,2048]{3,2,1,0:T(8,128)} %param.9) | copy-start | bytes 1572868
  79.9 23.4 %all-to-all-start = ((bf16[4,64,2048]{2,1,0:T(8,128)(2,1)}), bf16[4,64,2048]{2,1,0:T(8,128)(2,1)S(1)}, u32[]{:S(2)}, u32[]{:S(2)}) async-start(bf16[4,64,2048]{2,1,0:T(8,128)(2,1)} %get-tuple-element.37), calls=%async_computation | async-start | bytes 2097152 | tf_op jit(solution)/shard_map/all_to_all | solution.py:66
Sparse Core Ops, SparseCore 0:
  9.1 13.2 all-gather.2
  31.1 22.9 all-gather.4
where the time goes:
time: 112 us; the launch traced here: 111 us
  blocking collectives  37.6 us (34%)
  waiting for transfers between devices  32.4 us (29%)
  between operations  13.6 us (12%)
  local copies, waits for them, and re-layouts  12.5 us (11%)
  matrix products  8.98 us (8%)
  starting transfers between devices  3.69 us (3%)
  other arithmetic  2.52 us (2%)
    pmax x1, blocking collectives, on_device(): lax.pmax(offered.astype(jnp.bfloat16), ('dst', 'org')).astype(offered.dtype)  37.6 us
    all_to_all x1, waiting for transfers between devices, on_device(): lax.all_to_all(rounded, 'dst', split_axis=0, concat_axis=0, tiled=True)  19.7 us
    all_gather x1, waiting for transfers between devices, on_device(): every_state = lax.all_gather(value_now, 'st', axis=3, tiled=True)  12.6 us
    dot_general x4, matrix products, dense_anchor(): return jnp.dot(kernel_row, weights, preferred_element_type=jnp.float32)  8.98 us
    gather x1, local copies, waits for them, and re-layouts, on_device(): shifted = jnp.take(every_state, chosen, axis=3)  7.05 us
    all_to_all x1, starting transfers between devices, on_device(): lax.all_to_all(rounded, 'dst', split_axis=0, concat_axis=0, tiled=True)  3.65 us
    unnamed x13, local copies, waits for them, and re-layouts  2.52 us
  transfers between devices with their start and end apart: 3, of which 2 were waited for; matrix products, arithmetic and copies ran while one was open for 1% of the time, Pallas kernels for 0%

commit v1 on v0

v1 whole, which is shorter than its diff:
```python
import functools

import jax
import jax.numpy as jnp
from jax import lax
from jax.experimental import pallas as pl
from jax.experimental.pallas import tpu as pltpu
from jax.sharding import PartitionSpec as P

DISCOUNT = 0.95
FLOOR = -1e30
LANES = 128
CHUNKS = 1


def rows_to_lanes(block, first, count):
    return jnp.concatenate([block[first + i : first + i + 1, :] for i in range(count)], axis=1)


def lanes_to_rows(row, rows):
    count = row.shape[1] // LANES
    parts = [row[:, i * LANES : (i + 1) * LANES] for i in range(count)]
    if rows > count:
        parts.append(jnp.zeros((rows - count, LANES), row.dtype))
    return jnp.concatenate(parts, axis=0)


def place(high, low):
    d = lax.axis_index("dst")
    return d // low, d % low


def weigh_kernel(high, low, orig, widths, value_ref, cost_ref, *out_refs):
    plain_refs, keyed_refs, own_ref = out_refs[: len(widths)], out_refs[len(widths) : -1], out_refs[-1]
    my_high, my_low = place(high, low)
    my_orig = lax.axis_index("org")
    rows = value_ref.shape[0]
    cols = cost_ref.shape[2]

    def kernel_part(turn):
        target = (my_low + low - turn) % low
        parts = []
        for r in range(high):
            k = jnp.exp(-cost_ref[((my_high + r) % high) * low + target])
            turned = k
            for s in range(1, orig):
                turned = jnp.where(my_orig == s, pltpu.roll(k, cols - s * rows, 1), turned)
            parts.append(turned.astype(jnp.bfloat16))
        return parts

    for r, part in enumerate(kernel_part(0)):
        own_ref[:, r * cols : (r + 1) * cols] = part
    for turn in range(1, low):
        for r, part in enumerate(kernel_part(turn)):
            keyed_refs[turn - 1][:, r * cols : (r + 1) * cols] = part
    base = high * cols
    start = 0
    tops = []
    for c, width in enumerate(widths):
        v = value_ref[:, start : start + width]
        top = jnp.max(v, axis=0, keepdims=True).astype(jnp.bfloat16).astype(jnp.float32)
        tops.append(top)
        e = jnp.exp(v - top).astype(jnp.bfloat16)
        plain_refs[c][:, :width] = e
        if c == 0:
            for ref in keyed_refs:
                ref[:, base : base + width] = e
        start += width
    packed = lanes_to_rows(jnp.concatenate(tops, axis=1), rows).astype(jnp.bfloat16)
    plain_refs[0][:, widths[0] :] = packed
    for ref in keyed_refs:
        ref[:, base + widths[0] :] = packed


def weigh(high, low, orig, widths, value, cost):
    rows, states = value.shape
    base = high * cost.shape[2]
    shapes = [jax.ShapeDtypeStruct((rows, w + (LANES if c == 0 else 0)), jnp.bfloat16) for c, w in enumerate(widths)]
    shapes += [jax.ShapeDtypeStruct((rows, base + widths[0] + LANES), jnp.bfloat16)] * (low - 1)
    shapes += [jax.ShapeDtypeStruct((rows, base), jnp.bfloat16)]
    return pl.pallas_call(
        functools.partial(weigh_kernel, high, low, orig, widths),
        out_shape=shapes,
        cost_estimate=pl.CostEstimate(
            flops=4 * rows * states, bytes_accessed=8 * rows * states, transcendentals=rows * states
        ),
        name="weigh",
    )(value, cost)


def sums_kernel(high, low, orig, slots, chunk, widths, skips, turns, count_ref, list_ref, *refs):
    groups = low * orig
    rows = refs[0].shape[0]
    key_refs, top_refs = refs[:low], refs[low : low + groups]
    piece_refs, out_refs = refs[low + groups : low + 2 * groups], refs[low + 2 * groups :]
    width = widths[chunk]
    first = sum(widths[:chunk]) // LANES
    my_high, my_low = place(high, low)
    my_orig = lax.axis_index("org")
    tops = [ref[...].astype(jnp.float32) for ref in top_refs]
    for n, turn in enumerate(turns):
        anchor = (((my_high + turn) % high) * low + my_low) * orig + my_orig
        limit = count_ref[anchor]
        feasible = []
        for i in range(low):
            for j in range(orig):
                block = (my_high * low + (my_low + i) % low) * orig + (my_orig + j) % orig

                def hit(k, found):
                    return found | jnp.where((list_ref[anchor, k] == block) & (k < limit), 1, 0)

                feasible.append(lax.fori_loop(0, slots, hit, jnp.int32(0), unroll=slots <= 4) > 0)
        ceiling = functools.reduce(
            jnp.maximum, [jnp.where(f, t, FLOOR) for f, t in zip(feasible, tops)]
        )
        total = jnp.zeros((rows, width), jnp.float32)
        for i in range(low):
            for j in range(orig):
                b = i * orig + j
                scale = jnp.exp(jnp.where(feasible[b], tops[b] - ceiling, FLOOR))
                at = (turn * orig + j) * rows
                product = jnp.dot(
                    key_refs[i][:, at : at + rows],
                    piece_refs[b][:, skips[b] : skips[b] + width],
                    preferred_element_type=jnp.float32,
                )
                total += rows_to_lanes(scale, first, width // LANES) * product
        out_refs[n][:, :width] = total.astype(jnp.bfloat16)
        if chunk == 0:
            out_refs[n][:, width:] = ceiling.astype(jnp.bfloat16)


def sums(high, low, orig, chunk, widths, turns, row_counts, dest_blocks, own_key, gathered):
    rows = own_key.shape[0]
    base = own_key.shape[1]
    groups = low * orig
    smem = pl.BlockSpec(memory_space=pltpu.SMEM)
    keyed = [b // orig > 0 and b % orig == 0 for b in range(groups)]
    width = widths[chunk]
    args, specs = [row_counts, dest_blocks, own_key], [smem, smem, pl.BlockSpec((rows, base), lambda g: (0, 0))]
    skips = [base if chunk == 0 and k else 0 for k in keyed]
    for i in range(1, low):
        args.append(gathered[0][i * orig])
        specs.append(pl.BlockSpec((rows, base), lambda g: (0, 0)))
    for b in range(groups):
        at = (widths[0] + (base if keyed[b] else 0)) // LANES
        args.append(gathered[0][b])
        specs.append(pl.BlockSpec((rows, LANES), functools.partial(lambda at, g: (0, at), at)))
    for b in range(groups):
        args.append(gathered[chunk][b])
        specs.append(pl.BlockSpec(gathered[chunk][b].shape, lambda g: (0, 0)))
    extra = LANES if chunk == 0 else 0
    return pl.pallas_call(
        functools.partial(sums_kernel, high, low, orig, dest_blocks.shape[1], chunk, widths, skips, turns),
        grid=(1,),
        in_specs=specs,
        out_specs=[pl.BlockSpec((rows, width + extra), lambda g: (0, 0))] * len(turns),
        out_shape=[jax.ShapeDtypeStruct((rows, width + extra), jnp.bfloat16)] * len(turns),
        cost_estimate=pl.CostEstimate(
            flops=2 * rows * rows * width * groups * len(turns),
            bytes_accessed=2 * rows * width * (groups + len(turns)),
            transcendentals=groups * width,
        ),
        name="sums",
    )(*args)


def finish_kernel(high, halves, widths, low_size, tile, utility_ref, next_ref, *refs):
    out_ref = refs[-1]
    chunks = len(widths)
    rows, states = utility_ref.shape
    mine = lax.axis_index("st")

    def source(r, h):
        return refs[(r * halves + h) * chunks : (r * halves + h + 1) * chunks]

    pieces = states // low_size
    lefts = []
    tops = []
    for r in range(high):
        stack = []
        rows_of = []
        for h in range(halves):
            got = source(r, h)
            c = got[0][:, widths[0] :].astype(jnp.float32)
            for k in range(pieces):
                at = k * low_size
                chunk = 0
                while at >= widths[chunk]:
                    at -= widths[chunk]
                    chunk += 1
                stack.append(got[chunk][:, at : at + low_size])
                per = low_size // LANES
                rows_of.append(rows_to_lanes(c, k * per, per))
        lefts.append(jnp.concatenate(stack, axis=0))
        tops.append(jnp.concatenate(rows_of, axis=0).astype(jnp.bfloat16))
    for start in range(0, states, tile):
        nxt = next_ref[:, start : start + tile]
        high_part = nxt // low_size
        low_part = nxt % low_size
        onehot = jnp.where(
            lax.broadcasted_iota(jnp.int32, (low_size, tile), 0) == low_part, 1.0, 0.0
        ).astype(jnp.bfloat16)
        values, ceilings = [], []
        for r in range(high):
            every = jnp.dot(lefts[r], onehot, preferred_element_type=jnp.float32)
            every_top = jnp.dot(tops[r], onehot, preferred_element_type=jnp.float32)
            value = jnp.zeros((rows, tile), jnp.float32)
            ceiling = jnp.zeros((1, tile), jnp.float32)
            for h in range(halves):
                part = ((mine + h) % halves) * pieces
                for k in range(pieces):
                    n = h * pieces + k
                    here = high_part == part + k
                    value = jnp.where(here, every[n * rows : (n + 1) * rows, :], value)
                    ceiling = jnp.where(here, every_top[n : n + 1, :], ceiling)
            values.append(value)
            ceilings.append(ceiling)
        ceiling = functools.reduce(jnp.maximum, ceilings)
        merged = sum(v * jnp.exp(c - ceiling) for v, c in zip(values, ceilings))
        out_ref[:, start : start + tile] = utility_ref[:, start : start + tile] + DISCOUNT * (
            ceiling + jnp.log(merged)
        )


def finish(high, halves, widths, utility, chosen, sources):
    rows, states = utility.shape
    low_size = min(512, states)
    tile = min(512, states)
    flat = [a for per_turn in sources for per_half in per_turn for a in per_half]
    return pl.pallas_call(
        functools.partial(finish_kernel, high, halves, widths, low_size, tile),
        out_shape=jax.ShapeDtypeStruct((rows, states), jnp.float32),
        cost_estimate=pl.CostEstimate(
            flops=2 * rows * halves * states * states * high // 1,
            bytes_accessed=8 * rows * states,
            transcendentals=2 * rows * states,
        ),
        name="finish",
    )(utility, chosen, *flat)


def on_device(sizes, value_now, utility, move_costs, dest_blocks, row_counts, transition):
    dest, orig, halves = sizes
    low = 2 if dest % 2 == 0 else 1
    high = dest // low
    rows, states = value_now.shape[2:]
    widths = (states // CHUNKS,) * CHUNKS
    both = ("dst", "org")

    def index(h, l, o):
        return (h * low + l) * orig + o

    def gather(x, i, j):
        pairs = [
            (index(h, l, o), index(h, (l - i) % low, (o - j) % orig))
            for h in range(high)
            for l in range(low)
            for o in range(orig)
        ]
        return lax.ppermute(x, both, pairs)

    def onward(x, r):
        return lax.ppermute(x, "dst", [(h * low + l, ((h + r) % high) * low + l) for h in range(high) for l in range(low)])

    def across(x, h):
        return lax.ppermute(x, "st", [(s, (s - h) % halves) for s in range(halves)])

    cost = move_costs.reshape(move_costs.shape[0], rows, move_costs.shape[4])
    made = weigh(high, low, orig, widths, value_now.reshape(rows, states), cost)
    plain, keyed, own_key = made[:CHUNKS], made[CHUNKS:-1], made[-1]
    gathered = []
    for c in range(CHUNKS):
        row = []
        for i in range(low):
            for j in range(orig):
                x = keyed[i - 1] if c == 0 and i > 0 and j == 0 else plain[c]
                row.append(x if i == j == 0 else gather(x, i, j))
        gathered.append(row)
    step = functools.partial(sums, high, low, orig)
    rest = (row_counts, dest_blocks, own_key, gathered)
    local = [[None] * CHUNKS for _ in range(high)]
    for c in range(CHUNKS):
        if high > 1:
            sent = step(c, widths, tuple(range(1, high)), *rest)
            for r in range(1, high):
                local[r][c] = onward(sent[r - 1], r)
    for c in range(CHUNKS):
        local[0][c] = step(c, widths, (0,), *rest)[0]
    sources = [
        [[x if h == 0 else across(x, h) for x in local[r]] for h in range(halves)] for r in range(high)
    ]
    chosen = lax.dynamic_slice_in_dim(transition, lax.axis_index("st") * states, states).reshape(1, states)
    out = finish(high, halves, widths, utility.reshape(rows, states), chosen, sources)
    return out.reshape(value_now.shape)


def solution(mesh):
    sizes = (mesh.shape["dst"], mesh.shape["org"], mesh.shape["st"])
    return jax.shard_map(
        functools.partial(on_device, sizes),
        mesh=mesh,
        in_specs=(
            P(("draws", "dst"), "org", None, "st"),
            P(("draws", "dst"), "org", None, "st"),
            P("draws", "org", None, "dst", None),
            P(),
            P(),
            P(),
        ),
        out_specs=P(("draws", "dst"), "org", None, "st"),
        check_vma=False,
    )
```

time: 112 us -> 45.7 us (0.41)
  blocking collectives: 37.6 us -> 0 us
  between operations: 13.6 us -> 0.02 us
  Pallas kernels: 0 us -> 12.4 us
  local copies, waits for them, and re-layouts: 12.5 us -> 2.85 us
  waiting for transfers between devices: 32.4 us -> 23 us
  matrix products: 8.98 us -> 0 us
  starting transfers between devices: 3.69 us -> 7.18 us
  other arithmetic: 2.52 us -> 0 us
    pmax x1 -> x0, blocking collectives: 37.6 us -> none  [on_device(): lax.pmax(offered.astype(jnp.bfloat16), ('dst', 'org')).astype(offered.dtype)]
    ppermute x0 -> x6, waiting for transfers between devices: none -> 23 us  [the longest x3 13.2 us: gather(): return lax.ppermute(x, both, pairs)]
    all_to_all x1 -> x0, waiting for transfers between devices: 19.7 us -> none  [on_device(): lax.all_to_all(rounded, 'dst', split_axis=0, concat_axis=0, tiled=True)]
    all_gather x2 -> x0, waiting for transfers between devices: 12.7 us -> none  [the longest x1 12.6 us: on_device(): every_state = lax.all_gather(value_now, 'st', axis=3, tiled=True)]
    pallas_call x0 -> x4, Pallas kernels: none -> 12.4 us  [the longest x1 5.45 us: finish(): pl.pallas_call(functools.partial(finish_kernel, high, halves, widths, low...]
    dot_general x4 -> x0, matrix products: 8.98 us -> none  [dense_anchor(): return jnp.dot(kernel_row, weights, preferred_element_type=jnp.float32)]
    ppermute x0 -> x6, starting transfers between devices: none -> 7.18 us  [the longest x3 4.58 us: gather(): return lax.ppermute(x, both, pairs)]
    gather x1 -> x0, local copies, waits for them, and re-layouts: 7.05 us -> none  [on_device(): shifted = jnp.take(every_state, chosen, axis=3)]
  transfers between devices with their start and end apart: 3 -> 6, of which waited for: 2 -> 4; matrix products, arithmetic and copies ran while one was open for 1% -> 3% of each run, Pallas kernels for 0% -> 5%
where the time goes in v1:
time: 45.7 us; the launch traced here: 45.5 us
  waiting for transfers between devices  23 us (50%)
  Pallas kernels  12.4 us (27%)
  starting transfers between devices  7.18 us (16%)
  local copies, waits for them, and re-layouts  2.85 us (6%)
    ppermute x3, waiting for transfers between devices, gather(): return lax.ppermute(x, both, pairs)  13.2 us
    ppermute x1, waiting for transfers between devices, onward(): lax.ppermute(x, 'dst', [(h * low + l, (h + r) % high * low + l) for h in...  8.94 us
    pallas_call x1, Pallas kernels, finish(): pl.pallas_call(functools.partial(finish_kernel, high, halves, widths, low...  5.45 us
    pallas_call x2, Pallas kernels, sums(): pl.pallas_call(functools.partial(sums_kernel, high, low, orig, dest_block...  4.93 us
    ppermute x3, starting transfers between devices, gather(): return lax.ppermute(x, both, pairs)  4.58 us
    ppermute x1, starting transfers between devices, onward(): lax.ppermute(x, 'dst', [(h * low + l, (h + r) % high * low + l) for h in...  2.6 us
    unnamed x17, local copies, waits for them, and re-layouts  2.21 us
    pallas_call x1, Pallas kernels, weigh(): pl.pallas_call(functools.partial(weigh_kernel, high, low, orig, widths),...  2.04 us
  transfers between devices with their start and end apart: 6, of which 4 were waited for; matrix products, arithmetic and copies ran while one was open for 3% of the time, Pallas kernels for 5%

profile of v1, /device:TPU:0, one launch (start us, length us, event | category | flops | bytes accessed | tf_op | source)
XLA Modules:
  0.0 45.5 jit_solution(16595901207203605933)
XLA Ops:
  0.0 2.0 %weigh.1 = (bf16[64,2176]{1,0:T(8,128)(2,1)}, bf16[64,2432]{1,0:T(8,128)(2,1)}, bf16[64,256]{1,0:T(8,128)(2,1)}) custom-call(f32[64,2048]{1,0:T(8,128)} %bitcast.5, f32[4,64,128]{2,1,0:T(8,128)} %bitcast.6), custom_call_target="tpu_custom_call" | custom-call | flops 524288 | bytes 1048576 | tf_op jit(solution)/shard_map/weigh/pallas_call | solution.py:81
  2.0 0.0 copy-start.4
  2.0 3.1 %collective-permute-start = (bf16[64,2432]{1,0:T(8,128)(2,1)}, bf16[64,2432]{1,0:T(8,128)(2,1)S(1)}, u32[]{:S(2)}, u32[]{:S(2)}) collective-permute-start(bf16[64,2432]{1,0:T(8,128)(2,1)} %get-tuple-element.9), channel_id=1, source_target_pairs={{0,4},{2,6},{4,0},{6,2},{8,12},{10,14},{12,8},{14,10},{1,5},{3,7},... | collective-permute-start | bytes 933896 | tf_op jit(solution)/shard_map/ppermute | solution.py:261
  5.1 1.4 %collective-permute-start.2 = (bf16[64,2176]{1,0:T(8,128)(2,1)}, bf16[64,2176]{1,0:T(8,128)(2,1)S(1)}, u32[]{:S(2)}, u32[]{:S(2)}) collective-permute-start(bf16[64,2176]{1,0:T(8,128)(2,1)} %get-tuple-element.10.refs_2_.refs_6_), channel_id=1, source_target_pairs={{0,6},{2,4},{4,2},{6,0},{8,14},{10,12},{12,10},{14,8},{1,7},{3,5},... | collective-permute-start | bytes 835592 | tf_op jit(solution)/shard_map/ppermute | solution.py:261
  6.5 0.1 collective-permute-start.1
  6.6 0.0 copy-done.4
  6.6 0.7 %copy.7.list_ref = s32[8,3]{1,0:T(8,128)} copy(s32[8,3]{0,1:T(4,128)S(1)} %copy-done.4) | data formatting | bytes 192 | tf_op args[3]
  7.3 12.5 %collective-permute-done.2.refs_5_.refs_9_ = bf16[64,2176]{1,0:T(8,128)(2,1)S(1)} collective-permute-done((bf16[64,2176]{1,0:T(8,128)(2,1)}, bf16[64,2176]{1,0:T(8,128)(2,1)S(1)}, u32[]{:S(2)}, u32[]{:S(2)}) %collective-permute-start.2) | collective-permute-done | bytes 278560 | tf_op jit(solution)/shard_map/ppermute | solution.py:261
  19.8 0.0 copy-start.1
  19.8 0.7 %collective-permute-done.1.refs_3_.refs_7_ = bf16[64,2176]{1,0:T(8,128)(2,1)S(1)} collective-permute-done((bf16[64,2176]{1,0:T(8,128)(2,1)}, bf16[64,2176]{1,0:T(8,128)(2,1)S(1)}, u32[]{:S(2)}, u32[]{:S(2)}) %collective-permute-start.1) | collective-permute-done | bytes 278560 | tf_op jit(solution)/shard_map/ppermute | solution.py:261
  20.5 0.0 copy-start.2
  20.5 0.0 collective-permute-done.refs_1_.refs_4_.refs_8_
  20.5 0.0 copy-start
  20.5 0.0 copy-done.1
  20.5 0.7 %copy-done.2 = bf16[64,2176]{1,0:T(8,128)(2,1)} copy-done((bf16[64,2176]{1,0:T(8,128)(2,1)}, bf16[64,2176]{1,0:T(8,128)(2,1)S(1)}, u32[]{:S(2)}) %copy-start.2) | copy-done | bytes 278552
  21.2 0.1 copy-done
  21.3 2.5 %sums.3 = bf16[64,2176]{1,0:T(8,128)(2,1)} custom-call(s32[8]{0:T(128)} %count_ref.3, s32[8,3]{1,0:T(8,128)} %copy.7.list_ref, bf16[64,256]{1,0:T(8,128)(2,1)} %get-tuple-element.8.refs_0_, bf16[64,2432]{1,0:T(8,128)(2,1)} %copy-done, bf16[64,2176]{1,0:T(8,128)(2,1)} %get-tuple-element.10.refs_2_.refs_6_, bf16[64,2176]{1,0:T(8,128)(2,1)} %copy-done.2, ...), custom_call_target="tpu_custom_call" | custom-call | flops 67108864 | bytes 1310720 | tf_op jit(solution)/shard_map/sums/pallas_call | solution.py:153
  23.8 2.6 %collective-permute-start.4 = (bf16[64,2176]{1,0:T(8,128)(2,1)}, bf16[64,2176]{1,0:T(8,128)(2,1)S(1)}, u32[]{:S(2)}, u32[]{:S(2)}) collective-permute-start(bf16[64,2176]{1,0:T(8,128)(2,1)} %sums.3), channel_id=1, source_target_pairs={{0,8},{4,12},{8,0},{12,4},{1,9},{5,13},{9,1},{13,5},{2,10},{6,14},... | collective-permute-start | bytes 835592 | tf_op jit(solution)/shard_map/ppermute | solution.py:264
  26.4 0.0 copy-start.3
  26.4 2.5 %sums.2.refs_0_ = bf16[64,2176]{1,0:T(8,128)(2,1)} custom-call(s32[8]{0:T(128)} %count_ref.3, s32[8,3]{1,0:T(8,128)} %copy.7.list_ref, bf16[64,256]{1,0:T(8,128)(2,1)} %get-tuple-element.8.refs_0_, bf16[64,2432]{1,0:T(8,128)(2,1)} %copy-done, bf16[64,2176]{1,0:T(8,128)(2,1)} %get-tuple-element.10.refs_2_.refs_6_, bf16[64,2176]{1,0:T(8,128)(2,1)} %copy-done.2, ...), custom_call_target="tpu_custom_call" | custom-call | flops 67108864 | bytes 1310720 | tf_op jit(solution)/shard_map/sums/pallas_call | solution.py:153
  28.8 0.0 collective-permute-start.3
  28.8 8.9 %collective-permute-done.4.refs_2_ = bf16[64,2176]{1,0:T(8,128)(2,1)S(1)} collective-permute-done((bf16[64,2176]{1,0:T(8,128)(2,1)}, bf16[64,2176]{1,0:T(8,128)(2,1)S(1)}, u32[]{:S(2)}, u32[]{:S(2)}) %collective-permute-start.4) | collective-permute-done | bytes 278560 | tf_op jit(solution)/shard_map/ppermute | solution.py:264
  37.8 0.0 copy-start.5
  37.8 0.0 collective-permute-start.5
  37.8 0.0 copy-done.3
  37.8 0.6 %dynamic_slice.3 = s32[2048]{0:T(1024)} dynamic-slice(s32[4096]{0:T(1024)S(1)} %copy-done.3, s32[]{:T(128)S(6)} %select_n.3), dynamic_slice_sizes={2048} | dynamic-slice | bytes 16388 | tf_op jit(solution)/shard_map/dynamic_slice | solution.py:293
  38.4 0.0 collective-permute-done.3.refs_1_
  38.4 0.0 copy-start.6
  38.4 0.9 %collective-permute-done.5.refs_3_ = bf16[64,2176]{1,0:T(8,128)(2,1)S(1)} collective-permute-done((bf16[64,2176]{1,0:T(8,128)(2,1)S(1)}, bf16[64,2176]{1,0:T(8,128)(2,1)S(1)}, u32[]{:S(2)}, u32[]{:S(2)}) %collective-permute-start.5) | collective-permute-done | bytes 278560 | tf_op jit(solution)/shard_map/ppermute | solution.py:267
  39.3 0.0 copy-start.7
  39.3 0.0 copy-done.5
  39.3 0.0 copy-done.6
  39.3 0.7 %copy-done.7 = bf16[64,2176]{1,0:T(8,128)(2,1)} copy-done((bf16[64,2176]{1,0:T(8,128)(2,1)}, bf16[64,2176]{1,0:T(8,128)(2,1)S(1)}, u32[]{:S(2)}) %copy-start.7) | copy-done | bytes 278552
  40.1 5.5 %finish.1 = f32[64,2048]{1,0:T(8,128)} custom-call(f32[64,2048]{1,0:T(8,128)} %bitcast.8, s32[1,2048]{1,0:T(1,128)} %bitcast.7, bf16[64,2176]{1,0:T(8,128)(2,1)} %sums.2.refs_0_, bf16[64,2176]{1,0:T(8,128)(2,1)} %copy-done.6, bf16[64,2176]{1,0:T(8,128)(2,1)} %copy-done.5, bf16[64,2176]{1,0:T(8,128)(2,1)} %copy-done.7), custom_call_target="tpu_custom_call" | custom-call | flops 2147483648 | bytes 1048576 | tf_op jit(solution)/shard_map/finish/pallas_call | solution.py:231
Async XLA Ops:
  2.0 4.6 %copy-start.4 = (s32[8,3]{0,1:T(4,128)S(1)}, s32[8,3]{0,1:T(4,128)}, u32[]{:S(2)}) copy-start(s32[8,3]{0,1:T(4,128)} %param.9) | copy-start | bytes 292
  2.0 18.5 %collective-permute-start = (bf16[64,2432]{1,0:T(8,128)(2,1)}, bf16[64,2432]{1,0:T(8,128)(2,1)S(1)}, u32[]{:S(2)}, u32[]{:S(2)}) collective-permute-start(bf16[64,2432]{1,0:T(8,128)(2,1)} %get-tuple-element.9), channel_id=1, source_target_pairs={{0,4},{2,6},{4,0},{6,2},{8,12},{10,14},{12,8},{14,10},{1,5},{3,7},... | collective-permute-start | bytes 933896 | tf_op jit(solution)/shard_map/ppermute | solution.py:261
  5.1 14.7 %collective-permute-start.2 = (bf16[64,2176]{1,0:T(8,128)(2,1)}, bf16[64,2176]{1,0:T(8,128)(2,1)S(1)}, u32[]{:S(2)}, u32[]{:S(2)}) collective-permute-start(bf16[64,2176]{1,0:T(8,128)(2,1)} %get-tuple-element.10.refs_2_.refs_6_), channel_id=1, source_target_pairs={{0,6},{2,4},{4,2},{6,0},{8,14},{10,12},{12,10},{14,8},{1,7},{3,5},... | collective-permute-start | bytes 835592 | tf_op jit(solution)/shard_map/ppermute | solution.py:261
  6.5 14.0 %collective-permute-start.1 = (bf16[64,2176]{1,0:T(8,128)(2,1)}, bf16[64,2176]{1,0:T(8,128)(2,1)S(1)}, u32[]{:S(2)}, u32[]{:S(2)}) collective-permute-start(bf16[64,2176]{1,0:T(8,128)(2,1)} %get-tuple-element.10.refs_2_.refs_6_), channel_id=1, source_target_pairs={{0,2},{2,0},{4,6},{6,4},{8,10},{10,8},{12,14},{14,12},{1,3},{3,1},... | collective-permute-start | bytes 835592 | tf_op jit(solution)/shard_map/ppermute | solution.py:261
  19.8 0.7 %copy-start.1 = (bf16[64,2176]{1,0:T(8,128)(2,1)}, bf16[64,2176]{1,0:T(8,128)(2,1)S(1)}, u32[]{:S(2)}) copy-start(bf16[64,2176]{1,0:T(8,128)(2,1)S(1)} %collective-permute-done.2.refs_5_.refs_9_) | copy-start | bytes 835588
  20.5 0.7 %copy-start.2 = (bf16[64,2176]{1,0:T(8,128)(2,1)}, bf16[64,2176]{1,0:T(8,128)(2,1)S(1)}, u32[]{:S(2)}) copy-start(bf16[64,2176]{1,0:T(8,128)(2,1)S(1)} %collective-permute-done.1.refs_3_.refs_7_) | copy-start | bytes 835588
  20.5 0.8 %copy-start = (bf16[64,2432]{1,0:T(8,128)(2,1)}, bf16[64,2432]{1,0:T(8,128)(2,1)S(1)}, u32[]{:S(2)}) copy-start(bf16[64,2432]{1,0:T(8,128)(2,1)S(1)} %collective-permute-done.refs_1_.refs_4_.refs_8_) | copy-start | bytes 933892
  23.8 14.0 %collective-permute-start.4 = (bf16[64,2176]{1,0:T(8,128)(2,1)}, bf16[64,2176]{1,0:T(8,128)(2,1)S(1)}, u32[]{:S(2)}, u32[]{:S(2)}) collective-permute-start(bf16[64,2176]{1,0:T(8,128)(2,1)} %sums.3), channel_id=1, source_target_pairs={{0,8},{4,12},{8,0},{12,4},{1,9},{5,13},{9,1},{13,5},{2,10},{6,14},... | collective-permute-start | bytes 835592 | tf_op jit(solution)/shard_map/ppermute | solution.py:264
  26.4 11.4 %copy-start.3 = (s32[4096]{0:T(1024)S(1)}, s32[4096]{0:T(1024)}, u32[]{:S(2)}) copy-start(s32[4096]{0:T(1024)} %param.11) | copy-start | bytes 49156
  28.8 9.6 %collective-permute-start.3 = (bf16[64,2176]{1,0:T(8,128)(2,1)}, bf16[64,2176]{1,0:T(8,128)(2,1)S(1)}, u32[]{:S(2)}, u32[]{:S(2)}) collective-permute-start(bf16[64,2176]{1,0:T(8,128)(2,1)} %sums.2.refs_0_), channel_id=1, source_target_pairs={{0,1},{1,0},{2,3},{3,2},{4,5},{5,4},{6,7},{7,6},{8,9},{9,8},{10,11... | collective-permute-start | bytes 835592 | tf_op jit(solution)/shard_map/ppermute | solution.py:267
  37.8 1.6 %copy-start.5 = (bf16[64,2176]{1,0:T(8,128)(2,1)}, bf16[64,2176]{1,0:T(8,128)(2,1)S(1)}, u32[]{:S(2)}) copy-start(bf16[64,2176]{1,0:T(8,128)(2,1)S(1)} %collective-permute-done.4.refs_2_) | copy-start | bytes 835588
  37.8 1.6 %collective-permute-start.5 = (bf16[64,2176]{1,0:T(8,128)(2,1)S(1)}, bf16[64,2176]{1,0:T(8,128)(2,1)S(1)}, u32[]{:S(2)}, u32[]{:S(2)}) collective-permute-start(bf16[64,2176]{1,0:T(8,128)(2,1)S(1)} %collective-permute-done.4.refs_2_), channel_id=1, source_target_pairs={{0,1},{1,0},{2,3},{3,2},{4,5},{5,4},{6,7},{7,6},{8,9},{9,8},{10,11... | collective-permute-start | bytes 835592 | tf_op jit(solution)/shard_map/ppermute | solution.py:267
  38.4 0.9 %copy-start.6 = (bf16[64,2176]{1,0:T(8,128)(2,1)}, bf16[64,2176]{1,0:T(8,128)(2,1)S(1)}, u32[]{:S(2)}) copy-start(bf16[64,2176]{1,0:T(8,128)(2,1)S(1)} %collective-permute-done.3.refs_1_) | copy-start | bytes 835588
  39.3 0.7 %copy-start.7 = (bf16[64,2176]{1,0:T(8,128)(2,1)}, bf16[64,2176]{1,0:T(8,128)(2,1)S(1)}, u32[]{:S(2)}) copy-start(bf16[64,2176]{1,0:T(8,128)(2,1)S(1)} %collective-permute-done.5.refs_3_) | copy-start | bytes 835588

commit v2 on v1

v2 whole, which is shorter than its diff:
```python
import functools

import jax
import jax.numpy as jnp
from jax import lax
from jax.experimental import pallas as pl
from jax.experimental.pallas import tpu as pltpu
from jax.sharding import PartitionSpec as P


DISCOUNT = 0.95
FLOOR = -1e30
LANES = 128
CHUNKS = 2
LOW_BITS = 9
GRANT = 24 * 2**20
TILES = 4


def call(kernel, outs, flops, touched, args, smem=()):
    specs = [pl.BlockSpec(memory_space=pltpu.SMEM if n in smem else pltpu.VMEM) for n in range(len(args))]
    held = [a if n in smem else pltpu.with_memory_space_constraint(a, pltpu.VMEM) for n, a in enumerate(args)]
    return pl.pallas_call(
        kernel,
        in_specs=specs,
        out_specs=[pl.BlockSpec(memory_space=pltpu.VMEM)] * len(outs),
        out_shape=[pltpu.VMEM(shape, dtype) for shape, dtype in outs],
        compiler_params=pltpu.CompilerParams(vmem_limit_bytes=GRANT),
        cost_estimate=pl.CostEstimate(flops=flops, bytes_accessed=touched, transcendentals=0),
    )(*held)


def rows_to_lanes(block, first, count):
    return jnp.concatenate([block[first + i : first + i + 1, :] for i in range(count)], axis=1)


def lanes_to_rows(row, rows):
    count = row.shape[1] // LANES
    parts = [row[:, i * LANES : (i + 1) * LANES] for i in range(count)]
    if rows > count:
        parts.append(jnp.zeros((rows - count, LANES), row.dtype))
    return jnp.concatenate(parts, axis=0)


def place(low):
    d = lax.axis_index("dst")
    return d // low, d % low


def weigh_kernel(high, low, orig, widths, value_ref, cost_ref, *out_refs):
    plain_refs, keyed_refs, own_ref = out_refs[: len(widths)], out_refs[len(widths) : -1], out_refs[-1]
    my_high, my_low = place(low)
    my_orig = lax.axis_index("org")
    rows = value_ref.shape[0]
    cols = cost_ref.shape[2]

    def kernel_part(turn):
        target = (my_low + low - turn) % low
        parts = []
        for r in range(high):
            k = jnp.exp(-cost_ref[((my_high + r) % high) * low + target])
            turned = k
            for s in range(1, orig):
                turned = jnp.where(my_orig == s, pltpu.roll(k, cols - s * rows, 1), turned)
            parts.append(turned.astype(jnp.bfloat16))
        return parts

    for r, part in enumerate(kernel_part(0)):
        own_ref[:, r * cols : (r + 1) * cols] = part
    for turn in range(1, low):
        for r, part in enumerate(kernel_part(turn)):
            keyed_refs[turn - 1][:, r * cols : (r + 1) * cols] = part
    base = high * cols
    start = 0
    tops = []
    for c, width in enumerate(widths):
        v = value_ref[:, start : start + width]
        top = jnp.max(v, axis=0, keepdims=True).astype(jnp.bfloat16).astype(jnp.float32)
        tops.append(top)
        e = jnp.exp(v - top).astype(jnp.bfloat16)
        plain_refs[c][:, :width] = e
        if c == 0:
            for ref in keyed_refs:
                ref[:, base : base + width] = e
        start += width
    packed = lanes_to_rows(jnp.concatenate(tops, axis=1), rows).astype(jnp.bfloat16)
    plain_refs[0][:, widths[0] :] = packed
    for ref in keyed_refs:
        ref[:, base + widths[0] :] = packed


def weigh(high, low, orig, widths, value, cost):
    rows, states = value.shape
    base = high * cost.shape[2]
    outs = [((rows, w + (LANES if c == 0 else 0)), jnp.bfloat16) for c, w in enumerate(widths)]
    outs += [((rows, base + widths[0] + LANES), jnp.bfloat16)] * (low - 1)
    outs += [((rows, base), jnp.bfloat16)]
    kernel = functools.partial(weigh_kernel, high, low, orig, widths)
    return call(kernel, outs, 8 * rows * states, 8 * rows * states, (value, cost))


def sums_kernel(low, orig, chunk, widths, turns, open_ref, own_ref, *refs):
    groups = low * orig
    rows, base = own_ref.shape
    width = widths[chunk]
    first = sum(widths[:chunk]) // LANES
    skips = [base if b >= orig and b % orig == 0 else 0 for b in range(groups)]
    tops = [refs[b][:, skips[b] + widths[0] : skips[b] + widths[0] + LANES].astype(jnp.float32) for b in range(groups)]
    pieces = refs[:groups] if chunk == 0 else refs[groups : 2 * groups]
    out_refs = refs[-len(turns) :]
    for n, turn in enumerate(turns):
        feasible = [open_ref[turn * groups + b : turn * groups + b + 1, :] > 0.5 for b in range(groups)]
        ceiling = functools.reduce(jnp.maximum, [jnp.where(f, t, FLOOR) for f, t in zip(feasible, tops)])
        total = jnp.zeros((rows, width), jnp.float32)
        for i in range(low):
            key_ref = own_ref if i == 0 else refs[i * orig]
            for j in range(orig):
                b = i * orig + j
                scale = jnp.exp(jnp.where(feasible[b], tops[b] - ceiling, FLOOR))
                at = (turn * orig + j) * rows
                skip = skips[b] if chunk == 0 else 0
                product = jnp.dot(
                    key_ref[:, at : at + rows],
                    pieces[b][:, skip : skip + width],
                    preferred_element_type=jnp.float32,
                )
                total += rows_to_lanes(scale, first, width // LANES) * product
        out_refs[n][:, :width] = total.astype(jnp.bfloat16)
        if chunk == 0:
            out_refs[n][:, width:] = ceiling.astype(jnp.bfloat16)


def sums(low, orig, chunk, widths, turns, open_to, own_key, gathered):
    rows = own_key.shape[0]
    width = widths[chunk]
    groups = low * orig
    args = [open_to, own_key, *gathered[0]]
    if chunk > 0:
        args += gathered[chunk]
    outs = [((rows, width + (LANES if chunk == 0 else 0)), jnp.bfloat16)] * len(turns)
    kernel = functools.partial(sums_kernel, low, orig, chunk, widths, turns)
    flops = 2 * rows * rows * width * groups * len(turns)
    return call(kernel, outs, flops, 2 * rows * width * (groups + len(turns)), args)


def spot_kernel(high, low, orig, transition_ref, count_ref, list_ref, high_ref, onehot_ref, open_ref):
    nxt = transition_ref[pl.ds(lax.axis_index("st"), 1), :]
    high_ref[...] = lax.shift_right_logical(nxt, LOW_BITS)
    low_part = nxt & (onehot_ref.shape[0] - 1)
    rows = lax.broadcasted_iota(jnp.int32, onehot_ref.shape, 0)
    onehot_ref[...] = jnp.where(rows == low_part, 1.0, 0.0).astype(jnp.bfloat16)
    slots = list_ref.shape[1]
    my_high, my_low = place(low)
    my_orig = lax.axis_index("org")
    for turn in range(high):
        anchor = (((my_high + turn) % high) * low + my_low) * orig + my_orig
        limit = count_ref[anchor]
        for i in range(low):
            for j in range(orig):
                block = (my_high * low + (my_low + i) % low) * orig + (my_orig + j) % orig

                def hit(k, found):
                    return found | jnp.where((list_ref[anchor, k] == block) & (k < limit), 1, 0)

                found = lax.fori_loop(0, slots, hit, jnp.int32(0), unroll=slots <= 4)
                at = (turn * low + i) * orig + j
                open_ref[at : at + 1, :] = jnp.full((1, LANES), found.astype(jnp.float32))


def spot(high, low, orig, halves, transition, row_counts, dest_blocks):
    states = transition.shape[0] // halves
    size = 2**LOW_BITS
    outs = [
        ((1, states), jnp.int32),
        ((size, states), jnp.bfloat16),
        ((-(-high * low * orig // 8) * 8, LANES), jnp.float32),
    ]
    args = (transition.reshape(halves, states), row_counts, dest_blocks)
    kernel = functools.partial(spot_kernel, high, low, orig)
    return call(kernel, outs, 4 * size * states, 2 * size * states, args, smem=(1, 2))


def pick(halves, widths, chunks, where, onehot, states, got, value, ceiling):
    size = onehot.shape[0]
    rows = value.shape[0]
    per = size // LANES
    mine = lax.axis_index("st")
    stack, tops, parts = [], [], []
    for h in range(halves):
        part = ((mine + h) % halves) * (states // size)
        for chunk, ref in zip(chunks, got[h]):
            start = sum(widths[:chunk]) // size
            for k in range(widths[chunk] // size):
                stack.append(ref[:, k * size : (k + 1) * size])
                parts.append(part + start + k)
    every = jnp.dot(jnp.concatenate(stack, axis=0), onehot, preferred_element_type=jnp.float32)
    for n, part in enumerate(parts):
        value = jnp.where(where == part, every[n * rows : (n + 1) * rows, :], value)
    if chunks[0] == 0:
        for h in range(halves):
            c = got[h][0][:, widths[0] :].astype(jnp.float32)
            tops += [rows_to_lanes(c, k * per, per) for k in range(states // size)]
        every = jnp.dot(
            jnp.concatenate(tops, axis=0).astype(jnp.bfloat16), onehot, preferred_element_type=jnp.float32
        )
        for h in range(halves):
            part = ((mine + h) % halves) * (states // size)
            for k in range(states // size):
                n = h * (states // size) + k
                ceiling = jnp.where(where == part + k, every[n : n + 1, :], ceiling)
    return value, ceiling


def pick_kernel(halves, widths, chunks, where_ref, onehot_ref, *refs):
    value_ref, ceiling_ref = refs[-2:]
    got = [refs[h * len(chunks) : (h + 1) * len(chunks)] for h in range(halves)]
    rest = refs[halves * len(chunks) : -2]
    value = rest[0][...] if rest else jnp.zeros(value_ref.shape, jnp.float32)
    ceiling = rest[1][...] if rest else jnp.zeros(ceiling_ref.shape, jnp.float32)
    value_ref[...], ceiling_ref[...] = pick(
        halves, widths, chunks, where_ref[...], onehot_ref[...], where_ref.shape[1], got, value, ceiling
    )


def picked(halves, widths, chunks, marks, got, before=()):
    where, onehot = marks
    rows, states = got[0][0].shape[0], where.shape[1]
    outs = [((rows, states), jnp.float32), ((1, states), jnp.float32)]
    args = [where, onehot, *[x for per in got for x in per], *before]
    kernel = functools.partial(pick_kernel, halves, widths, chunks)
    width = sum(widths[c] for c in chunks)
    return call(kernel, outs, 2 * rows * states * width * halves, 4 * rows * states, args)


def finish_kernel(halves, widths, chunks, turns, tile, utility_ref, where_ref, onehot_ref, *refs):
    out_ref = refs[-1]
    here = pl.ds(pl.multiple_of(pl.program_id(0) * tile, tile), tile)
    count = halves * len(chunks)
    where, onehot = where_ref[:, here], onehot_ref[:, here]
    values, ceilings = [refs[0][:, here]], [refs[1][:, here]]
    refs = refs[2:-1]
    for _ in range(turns):
        got = [refs[h * len(chunks) : (h + 1) * len(chunks)] for h in range(halves)]
        refs = refs[count:]
        if chunks[0] > 0:
            value, ceiling = refs[0][:, here], refs[1][:, here]
            refs = refs[2:]
        else:
            value, ceiling = jnp.zeros(out_ref.shape, jnp.float32), jnp.zeros((1, tile), jnp.float32)
        value, ceiling = pick(halves, widths, chunks, where, onehot, where_ref.shape[1], got, value, ceiling)
        values.append(value)
        ceilings.append(ceiling)
    ceiling = functools.reduce(jnp.maximum, ceilings)
    merged = sum(v * jnp.exp(c - ceiling) for v, c in zip(values, ceilings))
    out_ref[...] = utility_ref[:, here] + DISCOUNT * (ceiling + jnp.log(merged))


def finish(halves, widths, chunks, utility, marks, own, others):
    rows, states = utility.shape
    tile = states // TILES
    args = [utility, *marks, *own]
    for got, before in others:
        args += [x for per in got for x in per]
        args += before
    kernel = functools.partial(finish_kernel, halves, widths, chunks, len(others), tile)
    flops = 2 * rows * states * states * halves
    return pl.pallas_call(
        kernel,
        grid=(TILES,),
        in_specs=[pl.BlockSpec(memory_space=pltpu.VMEM)] * len(args),
        out_specs=pl.BlockSpec((rows, tile), lambda n: (0, n)),
        out_shape=jax.ShapeDtypeStruct((rows, states), jnp.float32),
        compiler_params=pltpu.CompilerParams(vmem_limit_bytes=GRANT),
        cost_estimate=pl.CostEstimate(flops=flops, bytes_accessed=12 * rows * states, transcendentals=0),
        name="finish",
    )(*[pltpu.with_memory_space_constraint(a, pltpu.VMEM) for a in args])


def on_device(sizes, value_now, utility, move_costs, dest_blocks, row_counts, transition):
    dest, orig, halves = sizes
    low = 2 if dest % 2 == 0 else 1
    high = dest // low
    rows, states = value_now.shape[2:]
    widths = (states // CHUNKS,) * CHUNKS
    every = tuple(range(CHUNKS))
    both = ("dst", "org")

    def index(h, l, o):
        return (h * low + l) * orig + o

    def gather(x, i, j):
        pairs = [
            (index(h, l, o), index(h, (l - i) % low, (o - j) % orig))
            for h in range(high)
            for l in range(low)
            for o in range(orig)
        ]
        return lax.ppermute(x, both, pairs)

    def onward(x, r):
        pairs = [(h * low + l, ((h + r) % high) * low + l) for h in range(high) for l in range(low)]
        return lax.ppermute(x, "dst", pairs)

    def across(x):
        pairs = [[(s, (s - h) % halves) for s in range(halves)] for h in range(halves)]
        return [x if h == 0 else lax.ppermute(x, "st", pairs[h]) for h in range(halves)]

    def by_core(xs):
        return list(zip(*[across(x) for x in xs]))

    cost = move_costs.reshape(move_costs.shape[0], rows, move_costs.shape[4])
    made = weigh(high, low, orig, widths, value_now.reshape(rows, states), cost)
    plain, keyed, own_key = made[:CHUNKS], made[CHUNKS:-1], made[-1]
    gathered = []
    for c in every:
        row = []
        for i in range(low):
            for j in range(orig):
                x = keyed[i - 1] if c == 0 and i > 0 and j == 0 else plain[c]
                row.append(x if i == j == 0 else gather(x, i, j))
        gathered.append(row)
    *marks, open_to = spot(high, low, orig, halves, transition, row_counts, dest_blocks)
    step = functools.partial(sums, low, orig)
    rest = (open_to, own_key, gathered)
    turns = tuple(range(1, high))
    passed = []
    for c in every:
        sent = step(c, widths, turns, *rest) if turns else []
        passed.append([onward(x, r) for r, x in zip(turns, sent)])
    own = []
    for c in every:
        own += step(c, widths, (0,), *rest)
    own = by_core(own)
    own = picked(halves, widths, every, marks, own)
    others = []
    for n in range(len(turns)):
        before = ()
        for c in every[:-1]:
            got = by_core([passed[c][n]])
            before = picked(halves, widths, (c,), marks, got, before)
        others.append((by_core([passed[-1][n]]), before))
    out = finish(halves, widths, every[-1:], utility.reshape(rows, states), marks, own, others)
    return out.reshape(value_now.shape)


def solution(mesh):
    sizes = (mesh.shape["dst"], mesh.shape["org"], mesh.shape["st"])

    def body(*args):
        return on_device(sizes, *args)

    return jax.shard_map(
        body,
        mesh=mesh,
        in_specs=(
            P(("draws", "dst"), "org", None, "st"),
            P(("draws", "dst"), "org", None, "st"),
            P("draws", "org", None, "dst", None),
            P(),
            P(),
            P(),
        ),
        out_specs=P(("draws", "dst"), "org", None, "st"),
        check_vma=False,
    )
```

time: 45.7 us -> 36.3 us (0.79)
  waiting for transfers between devices: 23 us -> 10.1 us
  starting transfers between devices: 7.18 us -> 14.4 us
  Pallas kernels: 12.4 us -> 7.18 us
  local copies, waits for them, and re-layouts: 2.85 us -> 4.11 us
    ppermute x3 -> x6, waiting for transfers between devices: 13.2 us -> 3.23 us  [gather(): return lax.ppermute(x, both, pairs)]
    ppermute x3 -> x6, starting transfers between devices: 4.58 us -> 9.89 us  [gather(): return lax.ppermute(x, both, pairs)]
    pallas_call x4 -> x9, Pallas kernels: 12.4 us -> 7.18 us  [the longest x8 4.82 us: call(): pl.pallas_call(kernel, in_specs=specs, out_specs=[pl.BlockSpec(memory_spa...]
    ppermute x3 -> x6, waiting for transfers between devices: 9.84 us -> 6.88 us  [the longest x2 6.87 us: onward(): return lax.ppermute(x, 'dst', pairs)]
    ppermute x3 -> x6, starting transfers between devices: 2.6 us -> 4.51 us  [the longest x2 4.36 us: onward(): return lax.ppermute(x, 'dst', pairs)]
    unnamed x17 -> x9, local copies, waits for them, and re-layouts: 2.21 us -> 3.38 us
    reshape x0 -> x1, local copies, waits for them, and re-layouts: none -> 0.73 us  [spot(): args = (transition.reshape(halves, states), row_counts, dest_blocks)]
    dynamic_slice x1 -> x0, local copies, waits for them, and re-layouts: 0.64 us -> none  [on_device(): lax.dynamic_slice_in_dim(transition, lax.axis_index('st') * states, states)]
  transfers between devices with their start and end apart: 6 -> 12, of which waited for: 4 -> 4; matrix products, arithmetic and copies ran while one was open for 3% -> 4% of each run, Pallas kernels for 5% -> 13%
where the time goes in v2:
time: 36.3 us; the launch traced here: 35.9 us
  starting transfers between devices  14.4 us (40%)
  waiting for transfers between devices  10.1 us (28%)
  Pallas kernels  7.18 us (20%)
  local copies, waits for them, and re-layouts  4.11 us (11%)
    ppermute x6, starting transfers between devices, gather(): return lax.ppermute(x, both, pairs)  9.89 us
    ppermute x2, waiting for transfers between devices, onward(): return lax.ppermute(x, 'dst', pairs)  6.87 us
    pallas_call x8, Pallas kernels, call(): pl.pallas_call(kernel, in_specs=specs, out_specs=[pl.BlockSpec(memory_spa...  4.82 us
    ppermute x2, starting transfers between devices, onward(): return lax.ppermute(x, 'dst', pairs)  4.36 us
    unnamed x9, local copies, waits for them, and re-layouts  3.38 us
    ppermute x6, waiting for transfers between devices, gather(): return lax.ppermute(x, both, pairs)  3.23 us
    pallas_call x1, Pallas kernels, finish(): pl.pallas_call(kernel, grid=(TILES,), in_specs=[pl.BlockSpec(memory_space...  2.36 us
    reshape x1, local copies, waits for them, and re-layouts, spot(): args = (transition.reshape(halves, states), row_counts, dest_blocks)  0.73 us
  transfers between devices with their start and end apart: 12, of which 4 were waited for; matrix products, arithmetic and copies ran while one was open for 4% of the time, Pallas kernels for 13%

profile of v2, /device:TPU:0, one launch (start us, length us, event | category | flops | bytes accessed | tf_op | source)
XLA Modules:
  0.0 35.9 jit_solution(18256642636751491823)
XLA Ops:
  0.0 0.0 copy-start.1
  0.0 1.0 %copy-done.1 = f32[1,1,64,2048]{3,2,1,0:T(8,128)S(1)} copy-done((f32[1,1,64,2048]{3,2,1,0:T(8,128)S(1)}, f32[1,1,64,2048]{3,2,1,0:T(8,128)}, u32[]{:S(2)}) %copy-start.1) | copy-done | bytes 524312
  1.0 0.0 copy-start.2
  1.0 0.9 %copy-done.2 = f32[4,1,64,1,128]{4,3,2,1,0:T(1,128)S(1)} copy-done((f32[4,1,64,1,128]{4,3,2,1,0:T(1,128)S(1)}, f32[4,1,64,1,128]{4,3,2,1,0:T(1,128)}, u32[]{:S(2)}) %copy-start.2) | copy-done | bytes 131096
  1.9 0.2 shard_map.65
  2.1 4.0 %collective-permute-start.2 = (bf16[64,1152]{1,0:T(8,128)(2,1)S(1)}, bf16[64,1152]{1,0:T(8,128)(2,1)S(1)}, u32[]{:S(2)}, u32[]{:S(2)}) collective-permute-start(bf16[64,1152]{1,0:T(8,128)(2,1)S(1)} %get-tuple-element.20.refs_0_), channel_id=1, source_target_pairs={{0,6},{2,4},{4,2},{6,0},{8,14},{10,12},{12,10},{14,8},{1,7},{3,5},... | collective-permute-start | bytes 442376 | tf_op jit(solution)/shard_map/ppermute | solution.py:298
  6.1 0.4 %collective-permute-start.1 = (bf16[64,1408]{1,0:T(8,128)(2,1)S(1)}, bf16[64,1408]{1,0:T(8,128)(2,1)S(1)}, u32[]{:S(2)}, u32[]{:S(2)}) collective-permute-start(bf16[64,1408]{1,0:T(8,128)(2,1)S(1)} %get-tuple-element.21), channel_id=1, source_target_pairs={{0,4},{2,6},{4,0},{6,2},{8,12},{10,14},{12,8},{14,10},{1,5},{3,7},... | collective-permute-start | bytes 540680 | tf_op jit(solution)/shard_map/ppermute | solution.py:298
  6.6 0.2 collective-permute-start
  6.8 2.8 %collective-permute-start.5 = (bf16[64,1024]{1,0:T(8,128)(2,1)S(1)}, bf16[64,1024]{1,0:T(8,128)(2,1)S(1)}, u32[]{:S(2)}, u32[]{:S(2)}) collective-permute-start(bf16[64,1024]{1,0:T(8,128)(2,1)S(1)} %get-tuple-element.22.refs_4_), channel_id=1, source_target_pairs={{0,6},{2,4},{4,2},{6,0},{8,14},{10,12},{12,10},{14,8},{1,7},{3,5},... | collective-permute-start | bytes 393224 | tf_op jit(solution)/shard_map/ppermute | solution.py:298
  9.6 0.4 %collective-permute-start.4 = (bf16[64,1024]{1,0:T(8,128)(2,1)S(1)}, bf16[64,1024]{1,0:T(8,128)(2,1)S(1)}, u32[]{:S(2)}, u32[]{:S(2)}) collective-permute-start(bf16[64,1024]{1,0:T(8,128)(2,1)S(1)} %get-tuple-element.22.refs_4_), channel_id=1, source_target_pairs={{0,4},{2,6},{4,0},{6,2},{8,12},{10,14},{12,8},{14,10},{1,5},{3,7},... | collective-permute-start | bytes 393224 | tf_op jit(solution)/shard_map/ppermute | solution.py:298
  10.1 0.8 %collective-permute-done.2.refs_3_ = bf16[64,1152]{1,0:T(8,128)(2,1)S(1)} collective-permute-done((bf16[64,1152]{1,0:T(8,128)(2,1)S(1)}, bf16[64,1152]{1,0:T(8,128)(2,1)S(1)}, u32[]{:S(2)}, u32[]{:S(2)}) %collective-permute-start.2) | collective-permute-done | bytes 147488 | tf_op jit(solution)/shard_map/ppermute | solution.py:298
  10.8 1.9 %collective-permute-start.3 = (bf16[64,1024]{1,0:T(8,128)(2,1)S(1)}, bf16[64,1024]{1,0:T(8,128)(2,1)S(1)}, u32[]{:S(2)}, u32[]{:S(2)}) collective-permute-start(bf16[64,1024]{1,0:T(8,128)(2,1)S(1)} %get-tuple-element.22.refs_4_), channel_id=1, source_target_pairs={{0,2},{2,0},{4,6},{6,4},{8,10},{10,8},{12,14},{14,12},{1,3},{3,1},... | collective-permute-start | bytes 393224 | tf_op jit(solution)/shard_map/ppermute | solution.py:298
  12.8 0.8 %copy.7.list_ref = s32[8,3]{1,0:T(8,128)S(1)} copy(s32[8,3]{0,1:T(4,128)} %param.9) | data formatting | bytes 192 | tf_op args[3]
  13.5 0.7 %reshape.16.transition_ref = s32[2,2048]{1,0:T(2,128)S(1)} reshape(s32[4096]{0:T(1024)} %param.11) | data formatting | bytes 32768 | tf_op jit(solution)/shard_map/reshape | solution.py:178
  14.2 0.0 copy-start.3
  14.3 0.6 %copy-done.3 = s32[8]{0:T(128)S(1)} copy-done((s32[8]{0:T(128)S(1)}, s32[8]{0:T(128)}, u32[]{:S(2)}) %copy-start.3) | copy-done | bytes 56
  14.9 1.0 %shard_map.64 = (s32[1,2048]{1,0:T(1,128)S(1)}, bf16[512,2048]{1,0:T(8,128)(2,1)S(1)}, f32[8,128]{1,0:T(8,128)S(1)}) custom-call(s32[2,2048]{1,0:T(2,128)S(1)} %reshape.16.transition_ref, s32[8]{0:T(128)S(1)} %copy-done.3, s32[8,3]{1,0:T(8,128)S(1)} %copy.7.list_ref), custom_call_target="tpu_custom_call" | custom-call | flops 4194304 | bytes 2097152 | tf_op jit(solution)/shard_map/pallas_call | solution.py:23
  15.9 0.0 collective-permute-done.refs_1_
  15.9 0.0 collective-permute-done.1.refs_2_
  15.9 0.3 shard_map.70
  16.2 2.6 %collective-permute-start.10 = (bf16[64,1152]{1,0:T(8,128)(2,1)S(1)}, bf16[64,1152]{1,0:T(8,128)(2,1)S(1)}, u32[]{:S(2)}, u32[]{:S(2)}) collective-permute-start(bf16[64,1152]{1,0:T(8,128)(2,1)S(1)} %shard_map.70), channel_id=1, source_target_pairs={{0,8},{4,12},{8,0},{12,4},{1,9},{5,13},{9,1},{13,5},{2,10},{6,14},... | collective-permute-start | bytes 442376 | tf_op jit(solution)/shard_map/ppermute | solution.py:302
  18.9 0.3 shard_map.66.refs_0_
  19.2 0.1 collective-permute-start.6
  19.2 0.0 collective-permute-done.5.refs_7_
  19.2 2.5 %collective-permute-done.4.refs_6_ = bf16[64,1024]{1,0:T(8,128)(2,1)S(1)} collective-permute-done((bf16[64,1024]{1,0:T(8,128)(2,1)S(1)}, bf16[64,1024]{1,0:T(8,128)(2,1)S(1)}, u32[]{:S(2)}, u32[]{:S(2)}) %collective-permute-start.4) | collective-permute-done | bytes 131104 | tf_op jit(solution)/shard_map/ppermute | solution.py:298
  21.7 0.0 collective-permute-done.3.refs_5_
  21.7 0.3 shard_map.69
  22.0 1.7 %collective-permute-start.8 = (bf16[64,1024]{1,0:T(8,128)(2,1)S(1)}, bf16[64,1024]{1,0:T(8,128)(2,1)S(1)}, u32[]{:S(2)}, u32[]{:S(2)}) collective-permute-start(bf16[64,1024]{1,0:T(8,128)(2,1)S(1)} %shard_map.69), channel_id=1, source_target_pairs={{0,8},{4,12},{8,0},{12,4},{1,9},{5,13},{9,1},{13,5},{2,10},{6,14},... | collective-permute-start | bytes 393224 | tf_op jit(solution)/shard_map/ppermute | solution.py:302
  23.7 0.3 shard_map.67.refs_1_
  24.0 0.1 collective-permute-start.7
  24.1 4.5 %collective-permute-done.10.refs_0_ = bf16[64,1152]{1,0:T(8,128)(2,1)S(1)} collective-permute-done((bf16[64,1152]{1,0:T(8,128)(2,1)S(1)}, bf16[64,1152]{1,0:T(8,128)(2,1)S(1)}, u32[]{:S(2)}, u32[]{:S(2)}) %collective-permute-start.10) | collective-permute-done | bytes 147488 | tf_op jit(solution)/shard_map/ppermute | solution.py:302
  28.6 0.0 collective-permute-start.11
  28.6 2.4 %collective-permute-done.8.refs_2_ = bf16[64,1024]{1,0:T(8,128)(2,1)S(1)} collective-permute-done((bf16[64,1024]{1,0:T(8,128)(2,1)S(1)}, bf16[64,1024]{1,0:T(8,128)(2,1)S(1)}, u32[]{:S(2)}, u32[]{:S(2)}) %collective-permute-start.8) | collective-permute-done | bytes 131104 | tf_op jit(solution)/shard_map/ppermute | solution.py:302
  31.0 0.0 collective-permute-start.9
  31.0 0.0 collective-permute-done.7.refs_3_
  31.0 0.0 collective-permute-done.6.refs_2_
  31.0 1.5 %shard_map.68 = (f32[64,2048]{1,0:T(8,128)S(1)}, f32[1,2048]{1,0:T(1,128)S(1)}) custom-call(s32[1,2048]{1,0:T(1,128)S(1)} %get-tuple-element.16.where_ref, bf16[512,2048]{1,0:T(8,128)(2,1)S(1)} %get-tuple-element.17.onehot_ref, bf16[64,1152]{1,0:T(8,128)(2,1)S(1)} %shard_map.66.refs_0_, bf16[64,1024]{1,0:T(8,128)(2,1)S(1)} %shard_map.67.refs_1_, ...), custom_call_target="tpu_custom_call" | custom-call | flops 1073741824 | bytes 524288 | tf_op jit(solution)/shard_map/pallas_call | solution.py:23
  32.5 0.0 copy-start
  32.5 0.0 collective-permute-done.11.refs_1_
  32.6 1.0 %shard_map.71 = (f32[64,2048]{1,0:T(8,128)S(1)}, f32[1,2048]{1,0:T(1,128)S(1)}) custom-call(s32[1,2048]{1,0:T(1,128)S(1)} %get-tuple-element.16.where_ref, bf16[512,2048]{1,0:T(8,128)(2,1)S(1)} %get-tuple-element.17.onehot_ref, bf16[64,1152]{1,0:T(8,128)(2,1)S(1)} %collective-permute-done.10.refs_0_, bf16[64,1152]{1,0:T(8,128)(2,1)S(1)} %collective-permute-done.11.refs_1_), custom_call_target="tpu_custom_call" | custom-call | flops 536870912 | bytes 524288 | tf_op jit(solution)/shard_map/pallas_call | solution.py:23
  33.5 0.0 collective-permute-done.9.refs_3_
  33.6 0.0 copy-done
  33.6 2.4 %finish.1 = f32[64,2048]{1,0:T(8,128)} custom-call(f32[64,2048]{1,0:T(8,128)S(1)} %bitcast.4, s32[1,2048]{1,0:T(1,128)S(1)} %get-tuple-element.16.where_ref, bf16[512,2048]{1,0:T(8,128)(2,1)S(1)} %get-tuple-element.17.onehot_ref, f32[64,2048]{1,0:T(8,128)S(1)} %get-tuple-element.23.refs_0_, f32[1,2048]{1,0:T(1,128)S(1)} %get-tuple-element.24.refs_1_, ...), custom_call_target="tpu_custom_call" | custom-call | flops 1073741824 | bytes 1572864 | tf_op jit(solution)/shard_map/finish/pallas_call | solution.py:267
Async XLA Ops:
  0.0 1.0 %copy-start.1 = (f32[1,1,64,2048]{3,2,1,0:T(8,128)S(1)}, f32[1,1,64,2048]{3,2,1,0:T(8,128)}, u32[]{:S(2)}) copy-start(f32[1,1,64,2048]{3,2,1,0:T(8,128)} %param.6) | copy-start | bytes 1572868
  1.0 0.9 %copy-start.2 = (f32[4,1,64,1,128]{4,3,2,1,0:T(1,128)S(1)}, f32[4,1,64,1,128]{4,3,2,1,0:T(1,128)}, u32[]{:S(2)}) copy-start(f32[4,1,64,1,128]{4,3,2,1,0:T(1,128)} %param.8) | copy-start | bytes 393220
  2.1 8.7 %collective-permute-start.2 = (bf16[64,1152]{1,0:T(8,128)(2,1)S(1)}, bf16[64,1152]{1,0:T(8,128)(2,1)S(1)}, u32[]{:S(2)}, u32[]{:S(2)}) collective-permute-start(bf16[64,1152]{1,0:T(8,128)(2,1)S(1)} %get-tuple-element.20.refs_0_), channel_id=1, source_target_pairs={{0,6},{2,4},{4,2},{6,0},{8,14},{10,12},{12,10},{14,8},{1,7},{3,5},... | collective-permute-start | bytes 442376 | tf_op jit(solution)/shard_map/ppermute | solution.py:298
  6.1 9.7 %collective-permute-start.1 = (bf16[64,1408]{1,0:T(8,128)(2,1)S(1)}, bf16[64,1408]{1,0:T(8,128)(2,1)S(1)}, u32[]{:S(2)}, u32[]{:S(2)}) collective-permute-start(bf16[64,1408]{1,0:T(8,128)(2,1)S(1)} %get-tuple-element.21), channel_id=1, source_target_pairs={{0,4},{2,6},{4,0},{6,2},{8,12},{10,14},{12,8},{14,10},{1,5},{3,7},... | collective-permute-start | bytes 540680 | tf_op jit(solution)/shard_map/ppermute | solution.py:298
  6.6 9.3 %collective-permute-start = (bf16[64,1152]{1,0:T(8,128)(2,1)S(1)}, bf16[64,1152]{1,0:T(8,128)(2,1)S(1)}, u32[]{:S(2)}, u32[]{:S(2)}) collective-permute-start(bf16[64,1152]{1,0:T(8,128)(2,1)S(1)} %get-tuple-element.20.refs_0_), channel_id=1, source_target_pairs={{0,2},{2,0},{4,6},{6,4},{8,10},{10,8},{12,14},{14,12},{1,3},{3,1},... | collective-permute-start | bytes 442376 | tf_op jit(solution)/shard_map/ppermute | solution.py:298
  6.8 12.4 %collective-permute-start.5 = (bf16[64,1024]{1,0:T(8,128)(2,1)S(1)}, bf16[64,1024]{1,0:T(8,128)(2,1)S(1)}, u32[]{:S(2)}, u32[]{:S(2)}) collective-permute-start(bf16[64,1024]{1,0:T(8,128)(2,1)S(1)} %get-tuple-element.22.refs_4_), channel_id=1, source_target_pairs={{0,6},{2,4},{4,2},{6,0},{8,14},{10,12},{12,10},{14,8},{1,7},{3,5},... | collective-permute-start | bytes 393224 | tf_op jit(solution)/shard_map/ppermute | solution.py:298
  9.6 12.1 %collective-permute-start.4 = (bf16[64,1024]{1,0:T(8,128)(2,1)S(1)}, bf16[64,1024]{1,0:T(8,128)(2,1)S(1)}, u32[]{:S(2)}, u32[]{:S(2)}) collective-permute-start(bf16[64,1024]{1,0:T(8,128)(2,1)S(1)} %get-tuple-element.22.refs_4_), channel_id=1, source_target_pairs={{0,4},{2,6},{4,0},{6,2},{8,12},{10,14},{12,8},{14,10},{1,5},{3,7},... | collective-permute-start | bytes 393224 | tf_op jit(solution)/shard_map/ppermute | solution.py:298
  10.8 10.9 %collective-permute-start.3 = (bf16[64,1024]{1,0:T(8,128)(2,1)S(1)}, bf16[64,1024]{1,0:T(8,128)(2,1)S(1)}, u32[]{:S(2)}, u32[]{:S(2)}) collective-permute-start(bf16[64,1024]{1,0:T(8,128)(2,1)S(1)} %get-tuple-element.22.refs_4_), channel_id=1, source_target_pairs={{0,2},{2,0},{4,6},{6,4},{8,10},{10,8},{12,14},{14,12},{1,3},{3,1},... | collective-permute-start | bytes 393224 | tf_op jit(solution)/shard_map/ppermute | solution.py:298
  14.2 0.7 %copy-start.3 = (s32[8]{0:T(128)S(1)}, s32[8]{0:T(128)}, u32[]{:S(2)}) copy-start(s32[8]{0:T(128)} %count_ref.1) | copy-start | bytes 100
  16.2 12.4 %collective-permute-start.10 = (bf16[64,1152]{1,0:T(8,128)(2,1)S(1)}, bf16[64,1152]{1,0:T(8,128)(2,1)S(1)}, u32[]{:S(2)}, u32[]{:S(2)}) collective-permute-start(bf16[64,1152]{1,0:T(8,128)(2,1)S(1)} %shard_map.70), channel_id=1, source_target_pairs={{0,8},{4,12},{8,0},{12,4},{1,9},{5,13},{9,1},{13,5},{2,10},{6,14},... | collective-permute-start | bytes 442376 | tf_op jit(solution)/shard_map/ppermute | solution.py:302
  19.2 11.8 %collective-permute-start.6 = (bf16[64,1152]{1,0:T(8,128)(2,1)S(1)}, bf16[64,1152]{1,0:T(8,128)(2,1)S(1)}, u32[]{:S(2)}, u32[]{:S(2)}) collective-permute-start(bf16[64,1152]{1,0:T(8,128)(2,1)S(1)} %shard_map.66.refs_0_), channel_id=1, source_target_pairs={{0,1},{1,0},{2,3},{3,2},{4,5},{5,4},{6,7},{7,6},{8,9},{9,8},{10,11... | collective-permute-start | bytes 442376 | tf_op jit(solution)/shard_map/ppermute | solution.py:306
  22.0 9.0 %collective-permute-start.8 = (bf16[64,1024]{1,0:T(8,128)(2,1)S(1)}, bf16[64,1024]{1,0:T(8,128)(2,1)S(1)}, u32[]{:S(2)}, u32[]{:S(2)}) collective-permute-start(bf16[64,1024]{1,0:T(8,128)(2,1)S(1)} %shard_map.69), channel_id=1, source_target_pairs={{0,8},{4,12},{8,0},{12,4},{1,9},{5,13},{9,1},{13,5},{2,10},{6,14},... | collective-permute-start | bytes 393224 | tf_op jit(solution)/shard_map/ppermute | solution.py:302
  24.0 7.0 %collective-permute-start.7 = (bf16[64,1024]{1,0:T(8,128)(2,1)S(1)}, bf16[64,1024]{1,0:T(8,128)(2,1)S(1)}, u32[]{:S(2)}, u32[]{:S(2)}) collective-permute-start(bf16[64,1024]{1,0:T(8,128)(2,1)S(1)} %shard_map.67.refs_1_), channel_id=1, source_target_pairs={{0,1},{1,0},{2,3},{3,2},{4,5},{5,4},{6,7},{7,6},{8,9},{9,8},{10,11... | collective-permute-start | bytes 393224 | tf_op jit(solution)/shard_map/ppermute | solution.py:306
  28.6 3.9 %collective-permute-start.11 = (bf16[64,1152]{1,0:T(8,128)(2,1)S(1)}, bf16[64,1152]{1,0:T(8,128)(2,1)S(1)}, u32[]{:S(2)}, u32[]{:S(2)}) collective-permute-start(bf16[64,1152]{1,0:T(8,128)(2,1)S(1)} %collective-permute-done.10.refs_0_), channel_id=1, source_target_pairs={{0,1},{1,0},{2,3},{3,2},{4,5},{5,4},{6,7},{7,6},{8,9},{9,8},{10,11... | collective-permute-start | bytes 442376 | tf_op jit(solution)/shard_map/ppermute | solution.py:306
  31.0 2.6 %collective-permute-start.9 = (bf16[64,1024]{1,0:T(8,128)(2,1)S(1)}, bf16[64,1024]{1,0:T(8,128)(2,1)S(1)}, u32[]{:S(2)}, u32[]{:S(2)}) collective-permute-start(bf16[64,1024]{1,0:T(8,128)(2,1)S(1)} %collective-permute-done.8.refs_2_), channel_id=1, source_target_pairs={{0,1},{1,0},{2,3},{3,2},{4,5},{5,4},{6,7},{7,6},{8,9},{9,8},{10,11... | collective-permute-start | bytes 393224 | tf_op jit(solution)/shard_map/ppermute | solution.py:306
  32.5 1.0 %copy-start = (f32[1,1,64,2048]{3,2,1,0:T(8,128)S(1)}, f32[1,1,64,2048]{3,2,1,0:T(8,128)}, u32[]{:S(2)}) copy-start(f32[1,1,64,2048]{3,2,1,0:T(8,128)} %param.7) | copy-start | bytes 1572868

commit v3 on v2

--- a/solution.py
+++ b/solution.py
@@ -14,12 +14,16 @@
 CHUNKS = 2
 LOW_BITS = 9
 GRANT = 24 * 2**20
-TILES = 4
-
-
-def call(kernel, outs, flops, touched, args, smem=()):
+TILES = 2
+
+
+def call(kernel, outs, flops, touched, args, smem=(), fetched=()):
     specs = [pl.BlockSpec(memory_space=pltpu.SMEM if n in smem else pltpu.VMEM) for n in range(len(args))]
-    held = [a if n in smem else pltpu.with_memory_space_constraint(a, pltpu.VMEM) for n, a in enumerate(args)]
+    specs = [pl.BlockSpec() if n in fetched else spec for n, spec in enumerate(specs)]
+    spaces = {n: pltpu.HBM for n in fetched}
+    held = [
+        a if n in smem else pltpu.with_memory_space_constraint(a, spaces.get(n, pltpu.VMEM)) for n, a in enumerate(args)
+    ]
     return pl.pallas_call(
         kernel,
         in_specs=specs,
@@ -96,7 +100,7 @@
     outs += [((rows, base + widths[0] + LANES), jnp.bfloat16)] * (low - 1)
     outs += [((rows, base), jnp.bfloat16)]
     kernel = functools.partial(weigh_kernel, high, low, orig, widths)
-    return call(kernel, outs, 8 * rows * states, 8 * rows * states, (value, cost))
+    return call(kernel, outs, 8 * rows * states, 8 * rows * states, (value, cost), fetched=(0, 1))
 
 
 def sums_kernel(low, orig, chunk, widths, turns, open_ref, own_ref, *refs):
@@ -281,7 +285,8 @@
     low = 2 if dest % 2 == 0 else 1
     high = dest // low
     rows, states = value_now.shape[2:]
-    widths = (states // CHUNKS,) * CHUNKS
+    pieces = states // 2**LOW_BITS
+    widths = tuple((pieces + CHUNKS - 1 - c) // CHUNKS * 2**LOW_BITS for c in range(CHUNKS))
     every = tuple(range(CHUNKS))
     both = ("dst", "org")
 

time: 36.3 us -> 34.7 us (0.956)
  local copies, waits for them, and re-layouts: 4.11 us -> 2.16 us
  Pallas kernels: 7.18 us -> 7.63 us
    unnamed x9 -> x5, local copies, waits for them, and re-layouts: 3.38 us -> 1.43 us
    pallas_call x8, Pallas kernels: 4.82 us -> 5.94 us  [call(): pl.pallas_call(kernel, in_specs=specs, out_specs=[pl.BlockSpec(memory_spa...]
    pallas_call x1, Pallas kernels: 2.36 us -> 1.7 us  [finish(): pl.pallas_call(kernel, grid=(TILES,), in_specs=[pl.BlockSpec(memory_space...]
  transfers between devices with their start and end apart: 12 -> 12, of which waited for: 4 -> 4; matrix products, arithmetic and copies ran while one was open for 4% -> 4% of each run, Pallas kernels for 13% -> 14%
where the time goes in v3:
time: 34.7 us; the launch traced here: 34.4 us
  starting transfers between devices  14.4 us (41%)
  waiting for transfers between devices  10.1 us (29%)
  Pallas kernels  7.63 us (22%)
  local copies, waits for them, and re-layouts  2.16 us (6%)
    ppermute x6, starting transfers between devices, gather(): return lax.ppermute(x, both, pairs)  9.89 us
    ppermute x2, waiting for transfers between devices, onward(): return lax.ppermute(x, 'dst', pairs)  6.86 us
    pallas_call x8, Pallas kernels, call(): pl.pallas_call(kernel, in_specs=specs, out_specs=[pl.BlockSpec(memory_spa...  5.94 us
    ppermute x2, starting transfers between devices, onward(): return lax.ppermute(x, 'dst', pairs)  4.36 us
    ppermute x6, waiting for transfers between devices, gather(): return lax.ppermute(x, both, pairs)  3.24 us
    pallas_call x1, Pallas kernels, finish(): pl.pallas_call(kernel, grid=(TILES,), in_specs=[pl.BlockSpec(memory_space...  1.7 us
    unnamed x5, local copies, waits for them, and re-layouts  1.43 us
    reshape x1, local copies, waits for them, and re-layouts, spot(): args = (transition.reshape(halves, states), row_counts, dest_blocks)  0.73 us
  transfers between devices with their start and end apart: 12, of which 4 were waited for; matrix products, arithmetic and copies ran while one was open for 4% of the time, Pallas kernels for 14%

profile of v3, /device:TPU:0, one launch (start us, length us, event | category | flops | bytes accessed | tf_op | source)
XLA Modules:
  0.0 34.4 jit_solution(3868624672745710005)
XLA Ops:
  0.0 1.3 %shard_map.65 = (bf16[64,1152]{1,0:T(8,128)(2,1)S(1)}, bf16[64,1024]{1,0:T(8,128)(2,1)S(1)}, bf16[64,1408]{1,0:T(8,128)(2,1)S(1)}, bf16[64,256]{1,0:T(8,128)(2,1)S(1)}) custom-call(f32[64,2048]{1,0:T(8,128)} %bitcast.5, f32[4,64,128]{2,1,0:T(8,128)} %bitcast.6), custom_call_target="tpu_custom_call" | custom-call | flops 1048576 | bytes 1048576 | tf_op jit(solution)/shard_map/pallas_call | solution.py:27
  1.3 4.0 %collective-permute-start.2 = (bf16[64,1152]{1,0:T(8,128)(2,1)S(1)}, bf16[64,1152]{1,0:T(8,128)(2,1)S(1)}, u32[]{:S(2)}, u32[]{:S(2)}) collective-permute-start(bf16[64,1152]{1,0:T(8,128)(2,1)S(1)} %get-tuple-element.20.refs_0_), channel_id=1, source_target_pairs={{0,6},{2,4},{4,2},{6,0},{8,14},{10,12},{12,10},{14,8},{1,7},{3,5},... | collective-permute-start | bytes 442376 | tf_op jit(solution)/shard_map/ppermute | solution.py:303
  5.3 0.4 %collective-permute-start.1 = (bf16[64,1408]{1,0:T(8,128)(2,1)S(1)}, bf16[64,1408]{1,0:T(8,128)(2,1)S(1)}, u32[]{:S(2)}, u32[]{:S(2)}) collective-permute-start(bf16[64,1408]{1,0:T(8,128)(2,1)S(1)} %get-tuple-element.21), channel_id=1, source_target_pairs={{0,4},{2,6},{4,0},{6,2},{8,12},{10,14},{12,8},{14,10},{1,5},{3,7},... | collective-permute-start | bytes 540680 | tf_op jit(solution)/shard_map/ppermute | solution.py:303
  5.8 0.2 collective-permute-start
  6.0 2.8 %collective-permute-start.5 = (bf16[64,1024]{1,0:T(8,128)(2,1)S(1)}, bf16[64,1024]{1,0:T(8,128)(2,1)S(1)}, u32[]{:S(2)}, u32[]{:S(2)}) collective-permute-start(bf16[64,1024]{1,0:T(8,128)(2,1)S(1)} %get-tuple-element.22.refs_4_), channel_id=1, source_target_pairs={{0,6},{2,4},{4,2},{6,0},{8,14},{10,12},{12,10},{14,8},{1,7},{3,5},... | collective-permute-start | bytes 393224 | tf_op jit(solution)/shard_map/ppermute | solution.py:303
  8.8 0.4 %collective-permute-start.4 = (bf16[64,1024]{1,0:T(8,128)(2,1)S(1)}, bf16[64,1024]{1,0:T(8,128)(2,1)S(1)}, u32[]{:S(2)}, u32[]{:S(2)}) collective-permute-start(bf16[64,1024]{1,0:T(8,128)(2,1)S(1)} %get-tuple-element.22.refs_4_), channel_id=1, source_target_pairs={{0,4},{2,6},{4,0},{6,2},{8,12},{10,14},{12,8},{14,10},{1,5},{3,7},... | collective-permute-start | bytes 393224 | tf_op jit(solution)/shard_map/ppermute | solution.py:303
  9.3 0.8 %collective-permute-done.2.refs_3_ = bf16[64,1152]{1,0:T(8,128)(2,1)S(1)} collective-permute-done((bf16[64,1152]{1,0:T(8,128)(2,1)S(1)}, bf16[64,1152]{1,0:T(8,128)(2,1)S(1)}, u32[]{:S(2)}, u32[]{:S(2)}) %collective-permute-start.2) | collective-permute-done | bytes 147488 | tf_op jit(solution)/shard_map/ppermute | solution.py:303
  10.0 1.9 %collective-permute-start.3 = (bf16[64,1024]{1,0:T(8,128)(2,1)S(1)}, bf16[64,1024]{1,0:T(8,128)(2,1)S(1)}, u32[]{:S(2)}, u32[]{:S(2)}) collective-permute-start(bf16[64,1024]{1,0:T(8,128)(2,1)S(1)} %get-tuple-element.22.refs_4_), channel_id=1, source_target_pairs={{0,2},{2,0},{4,6},{6,4},{8,10},{10,8},{12,14},{14,12},{1,3},{3,1},... | collective-permute-start | bytes 393224 | tf_op jit(solution)/shard_map/ppermute | solution.py:303
  11.9 0.8 %copy.7.list_ref = s32[8,3]{1,0:T(8,128)S(1)} copy(s32[8,3]{0,1:T(4,128)} %param.9) | data formatting | bytes 192 | tf_op args[3]
  12.7 0.7 %reshape.16.transition_ref = s32[2,2048]{1,0:T(2,128)S(1)} reshape(s32[4096]{0:T(1024)} %param.11) | data formatting | bytes 32768 | tf_op jit(solution)/shard_map/reshape | solution.py:182
  13.4 0.0 copy-start.1
  13.4 0.6 %copy-done.1 = s32[8]{0:T(128)S(1)} copy-done((s32[8]{0:T(128)S(1)}, s32[8]{0:T(128)}, u32[]{:S(2)}) %copy-start.1) | copy-done | bytes 56
  14.1 1.0 %shard_map.64 = (s32[1,2048]{1,0:T(1,128)S(1)}, bf16[512,2048]{1,0:T(8,128)(2,1)S(1)}, f32[8,128]{1,0:T(8,128)S(1)}) custom-call(s32[2,2048]{1,0:T(2,128)S(1)} %reshape.16.transition_ref, s32[8]{0:T(128)S(1)} %copy-done.1, s32[8,3]{1,0:T(8,128)S(1)} %copy.7.list_ref), custom_call_target="tpu_custom_call" | custom-call | flops 4194304 | bytes 2097152 | tf_op jit(solution)/shard_map/pallas_call | solution.py:27
  15.0 0.0 collective-permute-done.refs_1_
  15.0 0.0 collective-permute-done.1.refs_2_
  15.1 0.3 shard_map.70
  15.4 2.6 %collective-permute-start.10 = (bf16[64,1152]{1,0:T(8,128)(2,1)S(1)}, bf16[64,1152]{1,0:T(8,128)(2,1)S(1)}, u32[]{:S(2)}, u32[]{:S(2)}) collective-permute-start(bf16[64,1152]{1,0:T(8,128)(2,1)S(1)} %shard_map.70), channel_id=1, source_target_pairs={{0,8},{4,12},{8,0},{12,4},{1,9},{5,13},{9,1},{13,5},{2,10},{6,14},... | collective-permute-start | bytes 442376 | tf_op jit(solution)/shard_map/ppermute | solution.py:307
  18.0 0.3 shard_map.66.refs_0_
  18.3 0.1 collective-permute-start.6
  18.4 0.0 collective-permute-done.5.refs_7_
  18.4 2.5 %collective-permute-done.4.refs_6_ = bf16[64,1024]{1,0:T(8,128)(2,1)S(1)} collective-permute-done((bf16[64,1024]{1,0:T(8,128)(2,1)S(1)}, bf16[64,1024]{1,0:T(8,128)(2,1)S(1)}, u32[]{:S(2)}, u32[]{:S(2)}) %collective-permute-start.4) | collective-permute-done | bytes 131104 | tf_op jit(solution)/shard_map/ppermute | solution.py:303
  20.9 0.0 collective-permute-done.3.refs_5_
  20.9 0.3 shard_map.69
  21.2 1.7 %collective-permute-start.8 = (bf16[64,1024]{1,0:T(8,128)(2,1)S(1)}, bf16[64,1024]{1,0:T(8,128)(2,1)S(1)}, u32[]{:S(2)}, u32[]{:S(2)}) collective-permute-start(bf16[64,1024]{1,0:T(8,128)(2,1)S(1)} %shard_map.69), channel_id=1, source_target_pairs={{0,8},{4,12},{8,0},{12,4},{1,9},{5,13},{9,1},{13,5},{2,10},{6,14},... | collective-permute-start | bytes 393224 | tf_op jit(solution)/shard_map/ppermute | solution.py:307
  22.9 0.3 shard_map.67.refs_1_
  23.2 0.1 collective-permute-start.7
  23.3 4.5 %collective-permute-done.10.refs_0_ = bf16[64,1152]{1,0:T(8,128)(2,1)S(1)} collective-permute-done((bf16[64,1152]{1,0:T(8,128)(2,1)S(1)}, bf16[64,1152]{1,0:T(8,128)(2,1)S(1)}, u32[]{:S(2)}, u32[]{:S(2)}) %collective-permute-start.10) | collective-permute-done | bytes 147488 | tf_op jit(solution)/shard_map/ppermute | solution.py:307
  27.8 0.0 collective-permute-start.11
  27.8 2.4 %collective-permute-done.8.refs_2_ = bf16[64,1024]{1,0:T(8,128)(2,1)S(1)} collective-permute-done((bf16[64,1024]{1,0:T(8,128)(2,1)S(1)}, bf16[64,1024]{1,0:T(8,128)(2,1)S(1)}, u32[]{:S(2)}, u32[]{:S(2)}) %collective-permute-start.8) | collective-permute-done | bytes 131104 | tf_op jit(solution)/shard_map/ppermute | solution.py:307
  30.2 0.0 collective-permute-start.9
  30.2 0.0 collective-permute-done.7.refs_3_
  30.2 0.0 collective-permute-done.6.refs_2_
  30.2 1.5 %shard_map.68 = (f32[64,2048]{1,0:T(8,128)S(1)}, f32[1,2048]{1,0:T(1,128)S(1)}) custom-call(s32[1,2048]{1,0:T(1,128)S(1)} %get-tuple-element.16.where_ref, bf16[512,2048]{1,0:T(8,128)(2,1)S(1)} %get-tuple-element.17.onehot_ref, bf16[64,1152]{1,0:T(8,128)(2,1)S(1)} %shard_map.66.refs_0_, bf16[64,1024]{1,0:T(8,128)(2,1)S(1)} %shard_map.67.refs_1_, ...), custom_call_target="tpu_custom_call" | custom-call | flops 1073741824 | bytes 524288 | tf_op jit(solution)/shard_map/pallas_call | solution.py:27
  31.7 0.0 copy-start
  31.7 0.0 collective-permute-done.11.refs_1_
  31.7 1.0 %shard_map.71 = (f32[64,2048]{1,0:T(8,128)S(1)}, f32[1,2048]{1,0:T(1,128)S(1)}) custom-call(s32[1,2048]{1,0:T(1,128)S(1)} %get-tuple-element.16.where_ref, bf16[512,2048]{1,0:T(8,128)(2,1)S(1)} %get-tuple-element.17.onehot_ref, bf16[64,1152]{1,0:T(8,128)(2,1)S(1)} %collective-permute-done.10.refs_0_, bf16[64,1152]{1,0:T(8,128)(2,1)S(1)} %collective-permute-done.11.refs_1_), custom_call_target="tpu_custom_call" | custom-call | flops 536870912 | bytes 524288 | tf_op jit(solution)/shard_map/pallas_call | solution.py:27
  32.7 0.0 collective-permute-done.9.refs_3_
  32.7 0.0 copy-done
  32.7 1.7 %finish.1 = f32[64,2048]{1,0:T(8,128)} custom-call(f32[64,2048]{1,0:T(8,128)S(1)} %bitcast.4, s32[1,2048]{1,0:T(1,128)S(1)} %get-tuple-element.16.where_ref, bf16[512,2048]{1,0:T(8,128)(2,1)S(1)} %get-tuple-element.17.onehot_ref, f32[64,2048]{1,0:T(8,128)S(1)} %get-tuple-element.23.refs_0_, f32[1,2048]{1,0:T(1,128)S(1)} %get-tuple-element.24.refs_1_, ...), custom_call_target="tpu_custom_call" | custom-call | flops 1073741824 | bytes 1572864 | tf_op jit(solution)/shard_map/finish/pallas_call | solution.py:271
Async XLA Ops:
  1.3 8.7 %collective-permute-start.2 = (bf16[64,1152]{1,0:T(8,128)(2,1)S(1)}, bf16[64,1152]{1,0:T(8,128)(2,1)S(1)}, u32[]{:S(2)}, u32[]{:S(2)}) collective-permute-start(bf16[64,1152]{1,0:T(8,128)(2,1)S(1)} %get-tuple-element.20.refs_0_), channel_id=1, source_target_pairs={{0,6},{2,4},{4,2},{6,0},{8,14},{10,12},{12,10},{14,8},{1,7},{3,5},... | collective-permute-start | bytes 442376 | tf_op jit(solution)/shard_map/ppermute | solution.py:303
  5.3 9.7 %collective-permute-start.1 = (bf16[64,1408]{1,0:T(8,128)(2,1)S(1)}, bf16[64,1408]{1,0:T(8,128)(2,1)S(1)}, u32[]{:S(2)}, u32[]{:S(2)}) collective-permute-start(bf16[64,1408]{1,0:T(8,128)(2,1)S(1)} %get-tuple-element.21), channel_id=1, source_target_pairs={{0,4},{2,6},{4,0},{6,2},{8,12},{10,14},{12,8},{14,10},{1,5},{3,7},... | collective-permute-start | bytes 540680 | tf_op jit(solution)/shard_map/ppermute | solution.py:303
  5.8 9.3 %collective-permute-start = (bf16[64,1152]{1,0:T(8,128)(2,1)S(1)}, bf16[64,1152]{1,0:T(8,128)(2,1)S(1)}, u32[]{:S(2)}, u32[]{:S(2)}) collective-permute-start(bf16[64,1152]{1,0:T(8,128)(2,1)S(1)} %get-tuple-element.20.refs_0_), channel_id=1, source_target_pairs={{0,2},{2,0},{4,6},{6,4},{8,10},{10,8},{12,14},{14,12},{1,3},{3,1},... | collective-permute-start | bytes 442376 | tf_op jit(solution)/shard_map/ppermute | solution.py:303
  6.0 12.4 %collective-permute-start.5 = (bf16[64,1024]{1,0:T(8,128)(2,1)S(1)}, bf16[64,1024]{1,0:T(8,128)(2,1)S(1)}, u32[]{:S(2)}, u32[]{:S(2)}) collective-permute-start(bf16[64,1024]{1,0:T(8,128)(2,1)S(1)} %get-tuple-element.22.refs_4_), channel_id=1, source_target_pairs={{0,6},{2,4},{4,2},{6,0},{8,14},{10,12},{12,10},{14,8},{1,7},{3,5},... | collective-permute-start | bytes 393224 | tf_op jit(solution)/shard_map/ppermute | solution.py:303
  8.8 12.1 %collective-permute-start.4 = (bf16[64,1024]{1,0:T(8,128)(2,1)S(1)}, bf16[64,1024]{1,0:T(8,128)(2,1)S(1)}, u32[]{:S(2)}, u32[]{:S(2)}) collective-permute-start(bf16[64,1024]{1,0:T(8,128)(2,1)S(1)} %get-tuple-element.22.refs_4_), channel_id=1, source_target_pairs={{0,4},{2,6},{4,0},{6,2},{8,12},{10,14},{12,8},{14,10},{1,5},{3,7},... | collective-permute-start | bytes 393224 | tf_op jit(solution)/shard_map/ppermute | solution.py:303
  10.0 10.9 %collective-permute-start.3 = (bf16[64,1024]{1,0:T(8,128)(2,1)S(1)}, bf16[64,1024]{1,0:T(8,128)(2,1)S(1)}, u32[]{:S(2)}, u32[]{:S(2)}) collective-permute-start(bf16[64,1024]{1,0:T(8,128)(2,1)S(1)} %get-tuple-element.22.refs_4_), channel_id=1, source_target_pairs={{0,2},{2,0},{4,6},{6,4},{8,10},{10,8},{12,14},{14,12},{1,3},{3,1},... | collective-permute-start | bytes 393224 | tf_op jit(solution)/shard_map/ppermute | solution.py:303
  13.4 0.7 %copy-start.1 = (s32[8]{0:T(128)S(1)}, s32[8]{0:T(128)}, u32[]{:S(2)}) copy-start(s32[8]{0:T(128)} %count_ref.1) | copy-start | bytes 100
  15.4 12.4 %collective-permute-start.10 = (bf16[64,1152]{1,0:T(8,128)(2,1)S(1)}, bf16[64,1152]{1,0:T(8,128)(2,1)S(1)}, u32[]{:S(2)}, u32[]{:S(2)}) collective-permute-start(bf16[64,1152]{1,0:T(8,128)(2,1)S(1)} %shard_map.70), channel_id=1, source_target_pairs={{0,8},{4,12},{8,0},{12,4},{1,9},{5,13},{9,1},{13,5},{2,10},{6,14},... | collective-permute-start | bytes 442376 | tf_op jit(solution)/shard_map/ppermute | solution.py:307
  18.3 11.8 %collective-permute-start.6 = (bf16[64,1152]{1,0:T(8,128)(2,1)S(1)}, bf16[64,1152]{1,0:T(8,128)(2,1)S(1)}, u32[]{:S(2)}, u32[]{:S(2)}) collective-permute-start(bf16[64,1152]{1,0:T(8,128)(2,1)S(1)} %shard_map.66.refs_0_), channel_id=1, source_target_pairs={{0,1},{1,0},{2,3},{3,2},{4,5},{5,4},{6,7},{7,6},{8,9},{9,8},{10,11... | collective-permute-start | bytes 442376 | tf_op jit(solution)/shard_map/ppermute | solution.py:311
  21.2 9.0 %collective-permute-start.8 = (bf16[64,1024]{1,0:T(8,128)(2,1)S(1)}, bf16[64,1024]{1,0:T(8,128)(2,1)S(1)}, u32[]{:S(2)}, u32[]{:S(2)}) collective-permute-start(bf16[64,1024]{1,0:T(8,128)(2,1)S(1)} %shard_map.69), channel_id=1, source_target_pairs={{0,8},{4,12},{8,0},{12,4},{1,9},{5,13},{9,1},{13,5},{2,10},{6,14},... | collective-permute-start | bytes 393224 | tf_op jit(solution)/shard_map/ppermute | solution.py:307
  23.2 6.9 %collective-permute-start.7 = (bf16[64,1024]{1,0:T(8,128)(2,1)S(1)}, bf16[64,1024]{1,0:T(8,128)(2,1)S(1)}, u32[]{:S(2)}, u32[]{:S(2)}) collective-permute-start(bf16[64,1024]{1,0:T(8,128)(2,1)S(1)} %shard_map.67.refs_1_), channel_id=1, source_target_pairs={{0,1},{1,0},{2,3},{3,2},{4,5},{5,4},{6,7},{7,6},{8,9},{9,8},{10,11... | collective-permute-start | bytes 393224 | tf_op jit(solution)/shard_map/ppermute | solution.py:311
  27.8 3.9 %collective-permute-start.11 = (bf16[64,1152]{1,0:T(8,128)(2,1)S(1)}, bf16[64,1152]{1,0:T(8,128)(2,1)S(1)}, u32[]{:S(2)}, u32[]{:S(2)}) collective-permute-start(bf16[64,1152]{1,0:T(8,128)(2,1)S(1)} %collective-permute-done.10.refs_0_), channel_id=1, source_target_pairs={{0,1},{1,0},{2,3},{3,2},{4,5},{5,4},{6,7},{7,6},{8,9},{9,8},{10,11... | collective-permute-start | bytes 442376 | tf_op jit(solution)/shard_map/ppermute | solution.py:311
  30.2 2.6 %collective-permute-start.9 = (bf16[64,1024]{1,0:T(8,128)(2,1)S(1)}, bf16[64,1024]{1,0:T(8,128)(2,1)S(1)}, u32[]{:S(2)}, u32[]{:S(2)}) collective-permute-start(bf16[64,1024]{1,0:T(8,128)(2,1)S(1)} %collective-permute-done.8.refs_2_), channel_id=1, source_target_pairs={{0,1},{1,0},{2,3},{3,2},{4,5},{5,4},{6,7},{7,6},{8,9},{9,8},{10,11... | collective-permute-start | bytes 393224 | tf_op jit(solution)/shard_map/ppermute | solution.py:311
  31.7 1.0 %copy-start = (f32[1,1,64,2048]{3,2,1,0:T(8,128)S(1)}, f32[1,1,64,2048]{3,2,1,0:T(8,128)}, u32[]{:S(2)}) copy-start(f32[1,1,64,2048]{3,2,1,0:T(8,128)} %param.7) | copy-start | bytes 1572868
